TPU v7x, 256 devices: a whole 4x4x8 slice. The times are simulated.
256 devices in a mesh: dp: 4 (over x), context: 32 (over y, z), head: 2 (over core).
Axes of the slice: x: 4, y: 4, z: 8, core: 2. Of those that a mesh axis runs over, the one named last changes fastest.
Arguments:
- tokens: bfloat16 [4, 2, 4096, 4096], P('dp', None, 'context', 'head'), may hold values from -7 to 7
- queries: bfloat16 [4, 2, 4096, 2048], P('dp', None, 'context', 'head'), may hold values from -160 to 160
- grad_out: bfloat16 [4, 2, 4096, 2048], P('dp', None, 'context', 'head'), may hold values from -6 to 6
- w_key: bfloat16 [4096, 256], P('context', 'head'), may hold values from -0.09375 to 0.09375
- w_value: bfloat16 [4096, 256], P('context', 'head'), may hold values from -0.09375 to 0.09375
- block_len: int32 [4], P('dp'), may hold values from 8 to 32, as said below
Outputs:
- grad_query: bfloat16 [4, 2, 4096, 2048], P('dp', None, 'context', 'head')
- grad_x: bfloat16 [4, 2, 4096, 4096], P('dp', None, 'context', 'head')
- grad_wkey: float32 [4096, 256], P('context', 'head')
- grad_wvalue: float32 [4096, 256], P('context', 'head')
Inputs may be any that keep to these rules, and one draw needn't show every extreme that they name: `block_len`: each entry is 8, 16 or 32.
All inputs are finite; a program needn't handle non-finite values.
Results may differ from a plain program's by a relative error of at most 0.025.
Values may be sent and summed in bfloat16 or wider, within the bound.
No kernel may reach another device: no remote copies, remote signals or barrier semaphores. Data moves between devices by JAX's collectives and lax.ppermute only.
A program may use at most 64 MiB of HBM per device.

v0:
```python
import math

import jax
import jax.numpy as jnp
from jax import lax
from jax.sharding import Mesh
from jax.sharding import PartitionSpec as P

HEAD_DIM = 128
CONTEXT = ("context_0", "context_1")


masked_score = -1e30


def joined_along(tiles, dim):
    lengths = list(tiles.shape[1:])
    lengths[dim] *= tiles.shape[0]
    return jnp.moveaxis(tiles, 0, dim).reshape(lengths)


def sent_to_all(array, axis):
    copies = jnp.broadcast_to(array, (lax.axis_size(axis), *array.shape))
    return lax.all_to_all(copies, axis, split_axis=0, concat_axis=0, tiled=True)


def gather_directly(array, axis, dim):
    return joined_along(sent_to_all(array, axis), dim)


def summed_rows(array, axes, dim):
    for axis in axes:
        array = lax.psum_scatter(array, axis, scatter_dimension=dim, tiled=True)
    return array


def split_up(array, dim, peers):
    lengths = array.shape
    tiles = array.reshape(*lengths[:dim], peers, lengths[dim] // peers, *lengths[dim + 1 :])
    return jnp.moveaxis(tiles, dim, 0)


def summed_on_arrival(array, axis, dim):
    peers = lax.axis_size(axis)
    tiles = lax.all_to_all(split_up(array, dim, peers), axis, 0, 0, tiled=True)
    return jnp.sum(tiles.astype(jnp.float32), axis=0)


def sum_by_axis(terms, axes):
    so_far = terms.astype(jnp.bfloat16)
    for axis in axes:
        so_far = lax.psum_scatter(so_far, axis, scatter_dimension=0, tiled=True)
    return so_far.astype(jnp.float32)


def over_copies(array, axis):
    everything = sent_to_all(array, axis)
    return jnp.sum(everything.astype(jnp.float32), axis=0)


def score_block(query_rows, key_rows, score_scale):
    return (
        jnp.einsum("ikgd,jkd->kgij", query_rows, key_rows, preferred_element_type=jnp.float32)
        * score_scale
    )


def visible_mask(query_pos, key_pos, block_size, strict):
    query_block = query_pos // block_size
    key_block = key_pos // block_size
    if strict:
        return key_block[None, :] < query_block[:, None]
    return key_block[None, :] <= query_block[:, None]


def forward_step(carried, query_rows, key_rows, value_rows, allowed_mask, score_scale):
    row_peak, row_total, weighted = carried
    logits = jnp.where(allowed_mask, score_block(query_rows, key_rows, score_scale), masked_score)
    new_peak = jnp.maximum(row_peak, jnp.max(logits, axis=-1))
    shrink = jnp.exp(row_peak - new_peak)
    weights = jnp.where(allowed_mask, jnp.exp(logits - new_peak[..., None]), 0.0)
    row_total = row_total * shrink + jnp.sum(weights, axis=-1)
    update = jnp.einsum(
        "kgij,jkd->kgid",
        weights.astype(jnp.bfloat16),
        value_rows,
        preferred_element_type=jnp.float32,
    )
    return (new_peak, row_total, weighted * shrink[..., None] + update)


def backward_step(
    query_rows, grad_rows, key_rows, value_rows, allowed_mask, log_total, row_delta, score_scale
):
    logits = jnp.where(allowed_mask, score_block(query_rows, key_rows, score_scale), masked_score)
    probs = jnp.exp(logits - log_total[..., None])
    probs_half = probs.astype(jnp.bfloat16)
    grad_probs = jnp.einsum(
        "ikgd,jkd->kgij", grad_rows, value_rows, preferred_element_type=jnp.float32
    )
    grad_logits = (probs * (grad_probs - row_delta[..., None])).astype(jnp.bfloat16)
    grad_rows_query = jnp.einsum(
        "kgij,jkd->ikgd", grad_logits, key_rows, preferred_element_type=jnp.float32
    )
    grad_key = (
        jnp.einsum("kgij,ikgd->jkd", grad_logits, query_rows, preferred_element_type=jnp.float32)
        * score_scale
    )
    grad_value = jnp.einsum(
        "kgij,ikgd->jkd", probs_half, grad_rows, preferred_element_type=jnp.float32
    )
    return (grad_rows_query, grad_key, grad_value)


def finish_rows(carried, grad_rows):
    row_peak, row_total, weighted = carried
    outputs = weighted / row_total[..., None]
    row_delta = jnp.einsum("ikgd,kgid->kgi", grad_rows.astype(jnp.float32), outputs)
    return (row_peak + jnp.log(row_total), row_delta)


def per_device(tokens, queries, grad_out, w_key, w_value, block_len):
    cycle_size = lax.axis_size(CONTEXT)
    my_index = lax.axis_index(CONTEXT)
    shard_rows = tokens.shape[2]
    kv_width = w_key.shape[1]
    kv_local = kv_width // HEAD_DIM
    query_width = queries.shape[3]
    group_size = query_width // HEAD_DIM // kv_local
    score_scale = 1.0 / math.sqrt(HEAD_DIM)
    block_size = block_len[0]
    local_pos = lax.iota(jnp.int32, shard_rows)
    span_rows = min(cycle_size * shard_rows, max(512, shard_rows))
    full_tokens = gather_directly(tokens[0].reshape(2 * shard_rows, tokens.shape[3]), "head", 1)
    weight_pair = jnp.concatenate([w_key, w_value], axis=1)
    columns = full_tokens
    projected = jnp.dot(
        columns,
        lax.all_gather(weight_pair, CONTEXT, axis=0, tiled=True),
        preferred_element_type=jnp.float32,
    ).astype(jnp.bfloat16)
    clean_pairs = projected[:shard_rows]
    q_clean = queries[0, 0].reshape(shard_rows, kv_local, group_size, HEAD_DIM)
    g_clean = grad_out[0, 0].reshape(shard_rows, kv_local, group_size, HEAD_DIM)
    noisy_bundle = jnp.concatenate([queries[0, 1], grad_out[0, 1], projected[shard_rows:]], axis=1)
    q_noisy = noisy_bundle[:, :query_width].reshape(shard_rows, kv_local, group_size, HEAD_DIM)
    g_noisy = noisy_bundle[:, query_width : 2 * query_width].reshape(
        shard_rows, kv_local, group_size, HEAD_DIM
    )
    k_noisy = noisy_bundle[:, 2 * query_width : 2 * query_width + kv_width].reshape(
        shard_rows, kv_local, HEAD_DIM
    )
    v_noisy = noisy_bundle[:, 2 * query_width + kv_width :].reshape(shard_rows, kv_local, HEAD_DIM)
    clean_pos = my_index * shard_rows + local_pos
    noisy_pos = my_index * shard_rows + local_pos
    own_block = local_pos // block_size
    same_block = own_block[None, :] == own_block[:, None]
    clean_limit = (my_index + 1) * shard_rows
    noisy_limit = (my_index + 1) * shard_rows
    state_shape = (kv_local, group_size, shard_rows)
    empty_state = (
        jnp.full(state_shape, masked_score, jnp.float32),
        jnp.zeros(state_shape, jnp.float32),
        jnp.zeros(state_shape + (HEAD_DIM,), jnp.float32),
    )
    noisy_start = forward_step(empty_state, q_noisy, k_noisy, v_noisy, same_block, score_scale)
    block_turns = (jnp.maximum(clean_limit, noisy_limit) + span_rows - 1) // span_rows

    def split_pairs(pair_rows):
        count_rows = pair_rows.shape[0]
        key_rows = pair_rows[:, :kv_width].reshape(count_rows, kv_local, HEAD_DIM)
        value_rows = pair_rows[:, kv_width:].reshape(count_rows, kv_local, HEAD_DIM)
        return (key_rows, value_rows)

    carried = (empty_state, noisy_start)
    pair_rows = gather_directly(clean_pairs, CONTEXT, 0)
    first_row = jnp.int32(0)
    key_rows, value_rows = split_pairs(pair_rows)
    key_pos = lax.iota(jnp.int32, pair_rows.shape[0])
    clean_mask = visible_mask(clean_pos, key_pos, block_size, False)
    noisy_mask = visible_mask(noisy_pos, key_pos, block_size, True)

    def clean_update():
        return forward_step(carried[0], q_clean, key_rows, value_rows, clean_mask, score_scale)

    def clean_keep():
        return carried[0]

    def noisy_update():
        return forward_step(carried[1], q_noisy, key_rows, value_rows, noisy_mask, score_scale)

    def noisy_keep():
        return carried[1]

    clean_state = lax.cond(first_row < clean_limit, clean_update, clean_keep)
    noisy_state = lax.cond(first_row < noisy_limit, noisy_update, noisy_keep)
    clean_lse, clean_delta = finish_rows(clean_state, g_clean)
    noisy_lse, noisy_delta = finish_rows(noisy_state, g_noisy)
    pairs_back = lax.all_gather(clean_pairs, CONTEXT, axis=0, tiled=True)
    query_zero = jnp.zeros((shard_rows, kv_local, group_size, HEAD_DIM), jnp.float32)

    def backward_turn(turn_index, carried):
        query_grads, pair_total = carried
        first_row = turn_index * span_rows
        pair_rows = lax.dynamic_slice_in_dim(pairs_back, first_row, span_rows, 0)
        key_rows, value_rows = split_pairs(pair_rows)
        key_pos = first_row + lax.iota(jnp.int32, span_rows)
        clean_mask = visible_mask(clean_pos, key_pos, block_size, False)
        noisy_mask = visible_mask(noisy_pos, key_pos, block_size, True)
        pair_zero = jnp.zeros((span_rows, kv_local, HEAD_DIM), jnp.float32)

        def clean_work():
            return backward_step(
                q_clean,
                g_clean,
                key_rows,
                value_rows,
                clean_mask,
                clean_lse,
                clean_delta,
                score_scale,
            )

        def noisy_work():
            return backward_step(
                q_noisy,
                g_noisy,
                key_rows,
                value_rows,
                noisy_mask,
                noisy_lse,
                noisy_delta,
                score_scale,
            )

        def no_work():
            return (query_zero, pair_zero, pair_zero)

        clean_dq, clean_dk, clean_dv = lax.cond(first_row < clean_limit, clean_work, no_work)
        noisy_dq, noisy_dk, noisy_dv = lax.cond(first_row < noisy_limit, noisy_work, no_work)
        pair_grads = jnp.concatenate(
            [
                (clean_dk + noisy_dk).reshape(span_rows, kv_width),
                (clean_dv + noisy_dv).reshape(span_rows, kv_width),
            ],
            axis=1,
        )
        previous = lax.dynamic_slice_in_dim(pair_total, first_row, span_rows, 0)
        pair_total = lax.dynamic_update_slice_in_dim(
            pair_total, previous + pair_grads, first_row, 0
        )
        return ((query_grads[0] + clean_dq, query_grads[1] + noisy_dq), pair_total)

    pair_empty = jnp.zeros((cycle_size * shard_rows, 2 * kv_width), jnp.float32)
    query_grads, pair_total = lax.fori_loop(
        0, block_turns, backward_turn, ((query_zero, query_zero), pair_empty)
    )
    clean_pair_grads = (
        summed_rows(pair_total.astype(jnp.bfloat16), CONTEXT, 0)
        .astype(jnp.float32)
        .astype(jnp.bfloat16)
    )
    own_dq, own_dk, own_dv = backward_step(
        q_noisy, g_noisy, k_noisy, v_noisy, same_block, noisy_lse, noisy_delta, score_scale
    )
    dq_clean = (query_grads[0] * score_scale).astype(jnp.bfloat16).reshape(shard_rows, query_width)
    dq_noisy = (
        ((query_grads[1] + own_dq) * score_scale)
        .astype(jnp.bfloat16)
        .reshape(shard_rows, query_width)
    )
    noisy_pair = jnp.concatenate(
        [own_dk.reshape(shard_rows, kv_width), own_dv.reshape(shard_rows, kv_width)], axis=1
    ).astype(jnp.bfloat16)
    return_bundle = jnp.concatenate([dq_noisy, noisy_pair], axis=1)
    dq_noisy = return_bundle[:, :query_width]
    noisy_pair = return_bundle[:, query_width:]
    pair_grads = jnp.concatenate([clean_pair_grads, noisy_pair], axis=0)
    input_terms = jnp.einsum(
        "tc,rc->tr",
        pair_grads,
        lax.all_gather(weight_pair, CONTEXT, axis=0, tiled=True),
        preferred_element_type=jnp.float32,
    )
    grad_x = (
        summed_on_arrival(input_terms.astype(jnp.bfloat16), "head", 1)
        .astype(jnp.bfloat16)
        .reshape(tokens.shape)
    )
    columns = full_tokens
    weight_local = sum_by_axis(
        jnp.einsum("tr,tc->rc", columns, pair_grads, preferred_element_type=jnp.float32), CONTEXT
    )
    weight_sums = over_copies(weight_local.astype(jnp.bfloat16), "dp").astype(jnp.float32)
    grad_query = jnp.stack([dq_clean, dq_noisy])[None]
    return (grad_query, grad_x, weight_sums[:, :kv_width], weight_sums[:, kv_width:])


def solution(mesh):
    torus = Mesh(
        mesh.devices.reshape(mesh.shape["dp"], 4, 8, mesh.shape["head"]),
        ("dp", "context_0", "context_1", "head"),
    )
    in_specs = (
        P("dp", None, CONTEXT, "head"),
        P("dp", None, CONTEXT, "head"),
        P("dp", None, CONTEXT, "head"),
        P(CONTEXT, "head"),
        P(CONTEXT, "head"),
        P("dp"),
    )
    out_specs = (
        P("dp", None, CONTEXT, "head"),
        P("dp", None, CONTEXT, "head"),
        P(CONTEXT, "head"),
        P(CONTEXT, "head"),
    )
    return jax.shard_map(
        per_device, mesh=torus, in_specs=in_specs, out_specs=out_specs, check_vma=False
    )
```

profile of v0, /device:TPU:1, one launch (start us, length us, event | category | flops | bytes accessed | tf_op | source)
XLA Modules:
  0.0 502.3 jit_solution(627499071341025403)
XLA Ops:
  10.3 8.3 %all_to_all.20 = bf16[2,256,2048]{1,2,0:T(8,128)(2,1)S(1)} all-to-all(bf16[2,256,2048]{1,2,0:T(8,128)(2,1)S(1)} %broadcast_in_dim.134), channel_id=1, replica_groups=mesh['dp'=4,'context_0'=4,'context_1'=8,'head'=2] {'head'}, dimensions={0} | all-to-all | bytes 4194304 | tf_op jit(solution)/shard_map/all_to_all | solution.py:24
  18.6 70.5 %all-gather.3.cloned.1.call-done = bf16[4096,256]{1,0:T(8,128)(2,1)} async-done(((bf16[128,256]{1,0:T(8,128)(2,1)}), bf16[4096,256]{1,0:T(8,128)(2,1)}) %all-gather.3.cloned.1.call-update) | async-done | bytes 2097168 | tf_op jit(solution)/shard_map/all_gather | solution.py:139
  93.1 5.2 %all-to-all-start.1 = ((bf16[32,128,256]{2,1,0:T(8,128)(2,1)}), bf16[32,128,256]{2,1,0:T(8,128)(2,1)}, u32[]{:S(2)}, u32[]{:S(2)}) async-start(bf16[32,128,256]{2,1,0:T(8,128)(2,1)} %broadcast_in_dim.135), calls=%async_computation.1 | async-start | bytes 4194304 | tf_op jit(solution)/shard_map/all_to_all | solution.py:24
  108.5 32.5 %all-to-all-done.1 = bf16[32,128,256]{2,1,0:T(8,128)(2,1)} async-done(((bf16[32,128,256]{2,1,0:T(8,128)(2,1)}), bf16[32,128,256]{2,1,0:T(8,128)(2,1)}, u32[]{:S(2)}, u32[]{:S(2)}) %all-to-all-start.1) | async-done | bytes 2097184 | tf_op jit(solution)/shard_map/all_to_all | solution.py:24
  141.0 3.1 slice_bitcast_fusion
  144.2 18.4 %conditional.5 = (f32[1,8,128]{2,1,0:T(8,128)}, f32[1,8,128]{2,1,0:T(8,128)S(1)}, f32[1,8,128,128]{3,2,1,0:T(8,128)S(1)}, f32[1,8,128]{2,1,0:T(8,128)}) conditional(s32[]{:T(128)} %convert_element_type.79, (f32[1,8,128]{2,1,0:T(8,128)}, f32[1,8,128]{2,1,0:T(8,128)S(1)}, f32[1,8,128,128]{3,2,1,0:T(8,128)S(1)}) %tuple.160, (s32[4096]{0:T(1024)S(1)}, ...), branch_computations={%region_6.7_spmd, %region_7.10_spmd} | conditional | flops 2202799104 | bytes 58019872 | solution.py:196
  146.3 3.7 fusion.25
  150.7 4.0 fusion.27
  156.0 6.0 %fusion.35 = f32[1,8,128,128]{3,2,1,0:T(8,128)S(1)} fusion(f32[4096,128,8]{1,0,2:T(8,128)S(1)} %get-tuple-element.709, f32[8,128]{1,0:T(8,128)S(1)} %bitcast.427, pred[128,4096]{0,1:T(8,128)(4,1)S(1)} %broadcast_compare_fusion.1, bf16[4096,1,128]{2,0,1:T(8,128)(2,1)} %get-tuple-element.377, f32[1,8,128,128]{3,2,1,0:T(8,128)S(1)} %get-tuple-element.376, ...), kind=kOutput, calls=%fused_computation.33 | convolution fusion | flops 1094975488 | bytes 19406848 | tf_op jit(solution)/shard_map/cond/branch_1_fun/kgij,jkd->kgid/dot_general | solution.py:83
  165.6 15.8 %conditional.4 = (f32[1,8,128]{2,1,0:T(8,128)S(1)}, f32[1,8,128]{2,1,0:T(8,128)S(1)}, f32[1,8,128,128]{3,2,1,0:T(8,128)S(1)}, f32[1,8,128]{2,1,0:T(8,128)S(1)}) conditional(s32[]{:T(128)} %convert_element_type.79, () %tuple.57, (s32[4096]{0:T(1024)S(1)}, s32[128,4096]{0,1:T(8,128)S(1)}, bf16[4096,1,128]{2,0,1:T(8,128)(2,1)}, ...), branch_computations={%region_0.1_spmd, %region_1.4_spmd} | conditional | flops 2202670080 | bytes 57479200 | solution.py:195
  167.5 3.8 fusion.4
  171.3 4.2 fusion.6
  175.5 5.9 %fusion.14 = f32[1,8,128,128]{3,2,1,0:T(8,128)S(1)} fusion(f32[4096,128,8]{1,0,2:T(8,128)S(1)} %get-tuple-element.707, f32[8,128]{1,0:T(8,128)S(1)} %get-tuple-element.705, pred[128,4096]{0,1:T(8,128)(4,1)S(1)} %broadcast_compare_fusion, bf16[4096,1,128]{2,0,1:T(8,128)(2,1)} %get-tuple-element.369, f32[8,128]{1,0:T(8,128)S(1)} %get-tuple-element.704), kind=kOutput, calls=%fused_computation.11 | convolution fusion | flops 1094844416 | bytes 18882560 | tf_op jit(solution)/shard_map/cond/branch_1_fun/kgij,jkd->kgid/dot_general | solution.py:83
  183.8 3.6 all-gather.5.cloned.1.call-done
  191.5 18.1 %while.20 = (s32[]{:T(128)}, f32[128,1,8,128]{3,0,2,1:T(8,128)}, f32[128,1,8,128]{3,0,2,1:T(8,128)}, f32[4096,256]{0,1:T(8,128)}, s32[]{:T(128)}, /*index=5*/s32...) while((s32[]{:T(128)}, f32[128,1,8,128]{3,0,2,1:T(8,128)}, ...), condition=%wide.region_15.16_spmd.clone.clone, body=%wide.region_10.15_spmd.clone.clone.sunk | while | flops 1350440704 | bytes 36462060 | solution.py:255
  194.3 4.5 conditional.13
  198.8 4.5 conditional.12
  209.6 4.0 convert_element_type.84
  213.6 161.6 %reduce-scatter.9.cloned.1.call-done = bf16[1024,256]{0,1:T(8,128)(2,1)} async-done(((bf16[4096,256]{0,1:T(8,128)(2,1)}), bf16[1024,256]{0,1:T(8,128)(2,1)}) %reduce-scatter.9.cloned.1.call-update) | async-done | bytes 524304 | tf_op jit(solution)/shard_map/reduce_scatter | solution.py:33
  378.4 31.6 %reduce-scatter.13.cloned.1.call-done = bf16[128,256]{1,0:T(8,128)(2,1)} async-done(((bf16[1024,256]{1,0:T(8,128)(2,1)}), bf16[128,256]{1,0:T(8,128)(2,1)}) %reduce-scatter.13.cloned.1.call-update) | async-done | bytes 65552
  413.1 35.8 %reduce-scatter.11.cloned.1.call-done = bf16[1024,256]{0,1:T(8,128)(2,1)} async-done(((bf16[4096,256]{0,1:T(8,128)(2,1)}), bf16[1024,256]{0,1:T(8,128)(2,1)}) %reduce-scatter.11.cloned.1.call-update) | async-done | bytes 524304 | tf_op jit(solution)/shard_map/reduce_scatter | solution.py:52
  455.2 5.7 %all_to_all.21 = bf16[2,256,2048]{2,1,0:T(8,128)(2,1)S(1)} all-to-all(bf16[2,256,2048]{2,1,0:T(8,128)(2,1)S(1)} %bitcast.403), channel_id=1, replica_groups=mesh['dp'=4,'context_0'=4,'context_1'=8,'head'=2] {'head'}, dimensions={0} | all-to-all | bytes 4194304 | tf_op jit(solution)/shard_map/all_to_all | solution.py:45
  460.9 22.8 %reduce-scatter.15.cloned.1.call-done = bf16[128,256]{1,0:T(8,128)(2,1)} async-done(((bf16[1024,256]{1,0:T(8,128)(2,1)}), bf16[128,256]{1,0:T(8,128)(2,1)}) %reduce-scatter.15.cloned.1.call-update) | async-done | bytes 65552 | tf_op jit(solution)/shard_map/reduce_scatter | solution.py:52
  485.3 4.0 all-to-all-start.3
  (144 shorter events, 70.8 us)
Async XLA Ops:
  7.2 81.9 %all-gather.3.cloned.1.call-start = ((), (), s32[]{:S(2)}) async-start(), calls=%async_computation.8 | async-start | bytes 2162688 | tf_op jit(solution)/shard_map/all_gather | solution.py:139
  18.6 74.5 %copy-start.4 = (bf16[2,256,2048]{1,2,0:T(8,128)(2,1)}, bf16[2,256,2048]{1,2,0:T(8,128)(2,1)S(1)}, u32[]{:S(2)}) copy-start(bf16[2,256,2048]{1,2,0:T(8,128)(2,1)S(1)} %all_to_all.20) | copy-start | bytes 6291460
  91.4 9.8 %copy-start.16 = (bf16[256,256]{0,1:T(8,128)(2,1)}, bf16[256,256]{0,1:T(8,128)(2,1)S(1)}, u32[]{:S(2)}) copy-start(bf16[256,256]{0,1:T(8,128)(2,1)S(1)} %fusion.92) | copy-start | bytes 393220
  91.4 8.3 %copy-start.15 = (bf16[1,2,128,1024]{3,2,1,0:T(8,128)(2,1)S(1)}, bf16[1,2,128,1024]{3,2,1,0:T(8,128)(2,1)}, u32[]{:S(2)}) copy-start(bf16[1,2,128,1024]{3,2,1,0:T(8,128)(2,1)} %param.17) | copy-start | bytes 1572868
  91.4 6.9 %copy-start.14 = (bf16[128,256]{0,1:T(8,128)(2,1)}, bf16[128,256]{0,1:T(8,128)(2,1)S(1)}, u32[]{:S(2)}) copy-start(bf16[128,256]{0,1:T(8,128)(2,1)S(1)} %slice.67) | copy-start | bytes 196612
  93.1 47.9 %all-to-all-start.1 = ((bf16[32,128,256]{2,1,0:T(8,128)(2,1)}), bf16[32,128,256]{2,1,0:T(8,128)(2,1)}, u32[]{:S(2)}, u32[]{:S(2)}) async-start(bf16[32,128,256]{2,1,0:T(8,128)(2,1)} %broadcast_in_dim.135), calls=%async_computation.1 | async-start | bytes 4194304 | tf_op jit(solution)/shard_map/all_to_all | solution.py:24
  98.3 89.1 %all-gather.5.cloned.1.call-start = ((), (), s32[]{:S(2)}) async-start(), calls=%async_computation.9 | async-start | bytes 2162688 | tf_op jit(solution)/shard_map/all_gather | solution.py:199
  99.0 276.1 %reduce-scatter.9.cloned.1.call-start = ((), (), s32[]{:S(2)}) async-start(), calls=%async_computation.10 | async-start | bytes 2621440 | tf_op jit(solution)/shard_map/reduce_scatter | solution.py:33
  100.0 44.3 %copy-start.8 = (bf16[1,1,128,1024]{2,3,1,0:T(8,128)(2,1)}, bf16[1,1,128,1024]{2,3,1,0:T(8,128)(2,1)S(1)}, u32[]{:S(2)}) copy-start(bf16[1,1,128,1024]{2,3,1,0:T(8,128)(2,1)S(1)} %copy.165) | copy-start | bytes 786436
  101.2 5.6 %copy-start.17 = (bf16[256,256]{0,1:T(8,128)(2,1)S(1)}, bf16[256,256]{0,1:T(8,128)(2,1)}, u32[]{:S(2)}) copy-start(bf16[256,256]{0,1:T(8,128)(2,1)} %copy-done.16) | copy-start | bytes 393220
  101.3 81.3 %copy-start.6 = (bf16[1,1,128,1024]{2,3,1,0:T(8,128)(2,1)}, bf16[1,1,128,1024]{2,3,1,0:T(8,128)(2,1)S(1)}, u32[]{:S(2)}) copy-start(bf16[1,1,128,1024]{2,3,1,0:T(8,128)(2,1)S(1)} %copy.166) | copy-start | bytes 786436
  141.0 3.2 copy-start.18
  209.5 168.0 %copy-start.3 = (f32[1,8,128,128]{2,3,1,0:T(8,128)S(1)}, f32[1,8,128,128]{2,3,1,0:T(8,128)}, u32[]{:S(2)}) copy-start(f32[1,8,128,128]{2,3,1,0:T(8,128)} %copy-done.2) | copy-start | bytes 1572868
  209.6 168.1 %copy-start.7 = (bf16[1,1,128,1024]{2,3,1,0:T(8,128)(2,1)S(1)}, bf16[1,1,128,1024]{2,3,1,0:T(8,128)(2,1)}, u32[]{:S(2)}) copy-start(bf16[1,1,128,1024]{2,3,1,0:T(8,128)(2,1)} %copy-done.6) | copy-start | bytes 786436
  209.6 168.3 %copy-start.9 = (bf16[1,1,128,1024]{2,3,1,0:T(8,128)(2,1)S(1)}, bf16[1,1,128,1024]{2,3,1,0:T(8,128)(2,1)}, u32[]{:S(2)}) copy-start(bf16[1,1,128,1024]{2,3,1,0:T(8,128)(2,1)} %copy-done.8) | copy-start | bytes 786436
  213.5 197.4 %copy-start.5 = (bf16[2,256,2048]{1,2,0:T(8,128)(2,1)S(1)}, bf16[2,256,2048]{1,2,0:T(8,128)(2,1)}, u32[]{:S(2)}) copy-start(bf16[2,256,2048]{1,2,0:T(8,128)(2,1)} %copy-done.4) | copy-start | bytes 6291460
  213.5 196.4 %reduce-scatter.13.cloned.1.call-start = ((), (), s32[]{:S(2)}) async-start(), calls=%async_computation.12 | async-start | bytes 589824
  377.3 71.6 %reduce-scatter.11.cloned.1.call-start = ((), (), s32[]{:S(2)}) async-start(), calls=%async_computation.11 | async-start | bytes 2621440 | tf_op jit(solution)/shard_map/reduce_scatter | solution.py:52
  378.4 72.6 %copy-start.1 = (f32[128,1,8,128]{3,0,2,1:T(8,128)S(1)}, f32[128,1,8,128]{3,0,2,1:T(8,128)}, u32[]{:S(2)}) copy-start(f32[128,1,8,128]{3,0,2,1:T(8,128)} %get-tuple-element.441) | copy-start | bytes 1572868
  410.9 41.1 %copy-start = (f32[128,1,8,128]{3,0,2,1:T(8,128)S(1)}, f32[128,1,8,128]{3,0,2,1:T(8,128)}, u32[]{:S(2)}) copy-start(f32[128,1,8,128]{3,0,2,1:T(8,128)} %get-tuple-element.440) | copy-start | bytes 1572868
  413.0 41.2 %copy-start.11 = (bf16[4096,256]{1,0:T(8,128)(2,1)S(1)}, bf16[4096,256]{1,0:T(8,128)(2,1)}, u32[]{:S(2)}) copy-start(bf16[4096,256]{1,0:T(8,128)(2,1)} %all-gather.3.cloned.1.call-done) | copy-start | bytes 6291460
  413.0 70.7 %reduce-scatter.15.cloned.1.call-start = ((), (), s32[]{:S(2)}) async-start(), calls=%async_computation.13 | async-start | bytes 589824 | tf_op jit(solution)/shard_map/reduce_scatter | solution.py:52
  455.0 34.4 %copy-start.13 = (bf16[128,1,8,128]{0,3,2,1:T(8,128)(2,1)S(1)}, bf16[128,1,8,128]{0,3,2,1:T(8,128)(2,1)}, u32[]{:S(2)}) copy-start(bf16[128,1,8,128]{0,3,2,1:T(8,128)(2,1)} %fusion.88) | copy-start | bytes 786436
  485.3 9.5 %all-to-all-start.3 = ((bf16[4,128,256]{2,1,0:T(8,128)(2,1)}), bf16[4,128,256]{2,1,0:T(8,128)(2,1)S(1)}, u32[]{:S(2)}, u32[]{:S(2)}) async-start(bf16[4,128,256]{2,1,0:T(8,128)(2,1)} %broadcast_in_dim.144), calls=%async_computation.5 | async-start | bytes 524288 | tf_op jit(solution)/shard_map/all_to_all | solution.py:24
  (4 other events, 9.2 us)
Sparse Core Ops, SparseCore 0:
  11.2 77.8 all-gather.2
  102.2 85.1 all-gather.4
  213.7 161.4 reduce-scatter.8
  377.7 32.2 reduce-scatter.12
  413.1 35.7 reduce-scatter.10
  451.4 32.2 reduce-scatter.14
where the time goes:
time: 511 us; the launch traced here: 502 us
  waiting for transfers between devices  362 us (71%)
  matrix products  37.9 us (7%)
  other arithmetic  33.4 us (7%)
  local copies, waits for them, and re-layouts  30.2 us (6%)
  between operations  15.2 us (3%)
  blocking collectives  14 us (3%)
  starting transfers between devices  9.64 us (2%)
    reduce_scatter x1, waiting for transfers between devices, summed_rows(): array = lax.psum_scatter(array, axis, scatter_dimension=dim, tiled=True)  162 us
    all_gather x1, waiting for transfers between devices, per_device(): lax.all_gather(weight_pair, CONTEXT, axis=0, tiled=True)  70.5 us
    reduce_scatter x2, waiting for transfers between devices, sum_by_axis(): so_far = lax.psum_scatter(so_far, axis, scatter_dimension=0, tiled=True)  58.6 us
    all_to_all x2, waiting for transfers between devices, sent_to_all(): return lax.all_to_all(copies, axis, split_axis=0, concat_axis=0, tiled=True)  35.1 us
    unnamed x7, waiting for transfers between devices  32.3 us
    dot_general x3, matrix products, forward_step(): jnp.einsum('kgij,jkd->kgid', weights.astype(jnp.bfloat16), value_rows, pr...  13 us
    dot_general x5, matrix products, score_block(): jnp.einsum('ikgd,jkd->kgij', query_rows, key_rows, preferred_element_type...  11.5 us
  transfers between devices with their start and end apart: 8, of which 8 were waited for; matrix products, arithmetic and copies ran while one was open for 12% of the time, Pallas kernels for 0%

commit v1 on v0

v1 whole, which is shorter than its diff:
```python
import math

import jax
import jax.numpy as jnp
from jax import lax
from jax.experimental import pallas as pl
from jax.experimental.pallas import tpu as pltpu
from jax.sharding import Mesh
from jax.sharding import PartitionSpec as P

HEAD_DIM = 128
CONTEXT = ("context_0", "context_1")
BF16 = jnp.bfloat16
F32 = jnp.float32
MASKED = -1e30
SCALE = 1.0 / math.sqrt(HEAD_DIM)
EXP_SCALE = math.log2(math.e) / math.sqrt(HEAD_DIM)
BLOCK = 256
CHUNKS = 4


def dot(left, right):
    return jnp.dot(left, right, preferred_element_type=F32)


def shifted(array, axis, step):
    size = lax.axis_size(axis)
    return lax.ppermute(array, axis, [(i, (i + step) % size) for i in range(size)])


def mirrored(array):
    size = lax.axis_size(CONTEXT)
    return lax.ppermute(array, CONTEXT, [(i, size - 1 - i) for i in range(size)])


def turned_over(array, axis):
    size = lax.axis_size(axis)
    return lax.ppermute(array, axis, [(i, size - 1 - i) for i in range(size)])


def swapped(array):
    return lax.ppermute(array, "head", [(0, 1), (1, 0)])


def gather_z(array):
    copies = jnp.broadcast_to(array, (lax.axis_size("context_1"), *array.shape))
    tiles = lax.all_to_all(copies, "context_1", 0, 0, tiled=True)
    return tiles.reshape(-1, *array.shape[1:])


def gather_ring(array, axis):
    half = array.shape[0] // 2
    before = shifted(array, axis, 1)
    after = shifted(array, axis, -1)
    far_low = shifted(before[:half], axis, 1)
    far_high = shifted(after[half:], axis, -1)
    return array, before, jnp.concatenate([far_low, far_high], axis=0), after


def reduce_ring(pieces, axis):
    own, before, far_low, far_high, after = pieces
    half = far_low.shape[0]
    got_low = shifted(far_low, axis, 1)
    got_high = shifted(far_high, axis, -1)
    up = jnp.concatenate(
        [(after[:half].astype(F32) + got_low.astype(F32)).astype(BF16), after[half:]], axis=0
    )
    down = jnp.concatenate(
        [before[:half], (before[half:].astype(F32) + got_high.astype(F32)).astype(BF16)], axis=0
    )
    from_before = shifted(up, axis, 1)
    from_after = shifted(down, axis, -1)
    return own.astype(F32) + from_before.astype(F32) + from_after.astype(F32)


def scatter_z(array):
    size = lax.axis_size("context_1")
    tiles = array.reshape(size, array.shape[0] // size, array.shape[1])
    tiles = lax.all_to_all(tiles, "context_1", 0, 0, tiled=True)
    return jnp.sum(tiles.astype(F32), axis=0)


def attention_kernel(
    info,
    q_clean,
    g_clean,
    q_noisy,
    g_noisy,
    kv_0,
    kv_1,
    kv_2,
    kv_3,
    kv_own,
    dq_clean,
    dq_noisy,
    out_0,
    out_1,
    out_2a,
    out_2b,
    out_3,
    out_own,
    kvs,
    qh,
    gh,
    qt,
    gt,
    weights,
    gprobs,
    weights_own,
    gprobs_own,
    peak,
    total,
    moment,
    used,
    used_own,
    dqt,
    acc,
):
    row_y = info[0]
    tile_clean = info[1]
    tile_noisy = info[2]
    shift = info[3]
    blocks_y = 4
    full_clean = tile_clean >> 1
    full_noisy = tile_noisy >> 1
    for part, source in enumerate((kv_0, kv_1, kv_2, kv_3)):
        place = ((row_y - part) & 3) * blocks_y
        for b in range(blocks_y):
            kvs[place + b] = source[b * BLOCK : (b + 1) * BLOCK, :]
    for stream, (q_ref, g_ref) in enumerate(((q_clean, g_clean), (q_noisy, g_noisy))):
        for h in range(2 * CHUNKS):
            at = slice((h % 2) * HEAD_DIM, (h % 2 + 1) * HEAD_DIM)
            for ref, rows, turned in ((q_ref, qh, qt), (g_ref, gh, gt)):
                tile = ref[:, h * HEAD_DIM : (h + 1) * HEAD_DIM]
                rows[stream, h // 2, at, :] = tile
                turned[stream, h // 2, :, at] = tile.T
    acc[...] = jnp.zeros_like(acc)

    lane = lax.broadcasted_iota(jnp.int32, (1, BLOCK), 1) & (HEAD_DIM - 1)

    def limits(tile, after):
        pos = tile * HEAD_DIM + lane
        return ((pos >> shift) + after) << shift

    def step_forward(stream, k, v, j, visible, first, save_w, save_g, save_used):
        s = dot(k, qt[stream, j])
        d = dot(v, gt[stream, j])
        if visible is not None:
            s = jnp.where(visible, s, MASKED)
        top = jnp.max(s, axis=0, keepdims=True)
        if first:
            new_peak = top
        else:
            old_peak = peak[stream, j]
            new_peak = jnp.maximum(old_peak, top)
            shrink = jnp.exp2((old_peak - new_peak) * EXP_SCALE)
        w = jnp.exp2((s - new_peak) * EXP_SCALE)
        sum_w = jnp.sum(w, axis=0, keepdims=True)
        sum_m = jnp.sum(w * d, axis=0, keepdims=True)
        if not first:
            sum_w = total[stream, j] * shrink + sum_w
            sum_m = moment[stream, j] * shrink + sum_m
        peak[stream, j] = new_peak
        total[stream, j] = sum_w
        moment[stream, j] = sum_m
        save_used(j, new_peak)
        save_w(j, w)
        save_g(j, d)

    def saver(ref, slot):
        def save(j, value):
            ref[slot, j] = value

        return save

    def forward_block(slot, stream, block, visible, first):
        k = kvs[block, :, :HEAD_DIM]
        v = kvs[block, :, HEAD_DIM:]
        for j in range(CHUNKS):
            step_forward(
                stream, k, v, j, visible, first,
                saver(weights, slot), saver(gprobs, slot), saver(used, slot),
            )

    def own_saver(ref):
        def save(j, value):
            ref[j] = value

        return save

    key_row = lax.broadcasted_iota(jnp.int32, (BLOCK, BLOCK), 0)
    own_row = lax.broadcasted_iota(jnp.int32, (HEAD_DIM, BLOCK), 0)
    same = (own_row >> shift) == (jnp.broadcast_to(lane, (HEAD_DIM, BLOCK)) >> shift)
    for j in range(CHUNKS):
        step_forward(
            1, kv_own[:, :HEAD_DIM], kv_own[:, HEAD_DIM:], j, same, True,
            own_saver(weights_own), own_saver(gprobs_own), own_saver(used_own),
        )
    forward_block(15, 0, full_clean, key_row + full_clean * BLOCK < limits(tile_clean, 1), True)
    forward_block(16, 1, full_noisy, key_row + full_noisy * BLOCK < limits(tile_noisy, 0), False)

    def place_of(slot):
        clean = slot < full_clean
        return jnp.where(clean, 0, 1), jnp.where(clean, slot, slot - full_clean)

    def forward_turn(slot, carry):
        stream, block = place_of(slot)
        forward_block(slot, stream, block, None, False)
        return carry

    lax.fori_loop(0, 15, forward_turn, 0)

    for stream in range(2):
        for j in range(CHUNKS):
            inverse = 1.0 / total[stream, j]
            total[stream, j] = inverse
            moment[stream, j] = moment[stream, j] * inverse
            dqt[stream, j] = jnp.zeros((HEAD_DIM, BLOCK), F32)

    def step_backward(stream, kt, j, w, d, seen):
        factor = jnp.exp2((seen - peak[stream, j]) * EXP_SCALE) * total[stream, j]
        p = w * factor
        ds = (p * (d - moment[stream, j])).astype(BF16)
        dv = dot(p.astype(BF16), gh[stream, j])
        dk = dot(ds, qh[stream, j])
        dqt[stream, j] += dot(kt, ds)
        return dk, dv

    def backward_block(slot, stream, block):
        kt = kvs[block, :, :HEAD_DIM].T
        dk = jnp.zeros((BLOCK, HEAD_DIM), F32)
        dv = jnp.zeros((BLOCK, HEAD_DIM), F32)
        for j in range(CHUNKS):
            more_k, more_v = step_backward(
                stream, kt, j, weights[slot, j], gprobs[slot, j], used[slot, j]
            )
            dk += more_k
            dv += more_v
        acc[block, :, :HEAD_DIM] += dk * SCALE
        acc[block, :, HEAD_DIM:] += dv

    kt_own = kv_own[:, :HEAD_DIM].T
    dk = jnp.zeros((HEAD_DIM, HEAD_DIM), F32)
    dv = jnp.zeros((HEAD_DIM, HEAD_DIM), F32)
    for j in range(CHUNKS):
        more_k, more_v = step_backward(1, kt_own, j, weights_own[j], gprobs_own[j], used_own[j])
        dk += more_k
        dv += more_v
    out_own[:, :HEAD_DIM] = (dk * SCALE).astype(BF16)
    out_own[:, HEAD_DIM:] = dv.astype(BF16)

    def backward_turn(slot, carry):
        stream, block = place_of(slot)
        backward_block(slot, stream, block)
        return carry

    lax.fori_loop(0, 15, backward_turn, 0)
    backward_block(15, 0, full_clean)
    backward_block(16, 1, full_noisy)

    for stream, ref in enumerate((dq_clean, dq_noisy)):
        for h in range(2 * CHUNKS):
            at = slice((h % 2) * HEAD_DIM, (h % 2 + 1) * HEAD_DIM)
            tile = dqt[stream, h // 2, :, at]
            ref[:, h * HEAD_DIM : (h + 1) * HEAD_DIM] = (tile.T * SCALE).astype(BF16)
    for part, refs in enumerate(((out_0,), (out_1,), (out_2a, out_2b), (out_3,))):
        place = ((row_y - part) & 3) * blocks_y
        each = blocks_y // len(refs)
        for b in range(blocks_y):
            at = (b % each) * BLOCK
            refs[b // each][at : at + BLOCK, :] = acc[place + b].astype(BF16)


def attention(info, q_clean, g_clean, q_noisy, g_noisy, pieces, kv_own):
    rows, width = q_clean.shape
    span, kv_width = pieces[0].shape
    vmem = pl.BlockSpec(memory_space=pltpu.VMEM)
    shape = jax.ShapeDtypeStruct
    slots = 17
    return pl.pallas_call(
        attention_kernel,
        out_shape=(
            shape((rows, width), BF16),
            shape((rows, width), BF16),
            shape((span, kv_width), BF16),
            shape((span, kv_width), BF16),
            shape((span // 2, kv_width), BF16),
            shape((span // 2, kv_width), BF16),
            shape((span, kv_width), BF16),
            shape((rows, kv_width), BF16),
        ),
        in_specs=[pl.BlockSpec(memory_space=pltpu.SMEM)] + [vmem] * 9,
        out_specs=(vmem,) * 8,
        scratch_shapes=[
            pltpu.VMEM((16, BLOCK, kv_width), BF16),
            pltpu.VMEM((2, CHUNKS, BLOCK, HEAD_DIM), BF16),
            pltpu.VMEM((2, CHUNKS, BLOCK, HEAD_DIM), BF16),
            pltpu.VMEM((2, CHUNKS, HEAD_DIM, BLOCK), BF16),
            pltpu.VMEM((2, CHUNKS, HEAD_DIM, BLOCK), BF16),
            pltpu.VMEM((slots, CHUNKS, BLOCK, BLOCK), F32),
            pltpu.VMEM((slots, CHUNKS, BLOCK, BLOCK), F32),
            pltpu.VMEM((CHUNKS, HEAD_DIM, BLOCK), F32),
            pltpu.VMEM((CHUNKS, HEAD_DIM, BLOCK), F32),
            pltpu.VMEM((2, CHUNKS, 1, BLOCK), F32),
            pltpu.VMEM((2, CHUNKS, 1, BLOCK), F32),
            pltpu.VMEM((2, CHUNKS, 1, BLOCK), F32),
            pltpu.VMEM((slots, CHUNKS, 1, BLOCK), F32),
            pltpu.VMEM((CHUNKS, 1, BLOCK), F32),
            pltpu.VMEM((2, CHUNKS, HEAD_DIM, BLOCK), F32),
            pltpu.VMEM((16, BLOCK, kv_width), F32),
        ],
        compiler_params=pltpu.CompilerParams(vmem_limit_bytes=60 * 1024 * 1024),
    )(info, q_clean, g_clean, q_noisy, g_noisy, *pieces, kv_own)


def in_place_order(pieces, row_y):
    stacked = jnp.stack(pieces)
    ordered = [
        lax.dynamic_index_in_dim(stacked, (row_y - part) & 3, 0, keepdims=False)
        for part in range(4)
    ]
    return jnp.concatenate(ordered, axis=0)


def per_device(tokens, queries, grad_out, w_key, w_value, block_len):
    row_y = lax.axis_index("context_0")
    my_index = lax.axis_index(CONTEXT)
    head = lax.axis_index("head")
    size = lax.axis_size(CONTEXT)
    shard_rows = tokens.shape[2]
    features = tokens.shape[3]
    kv_width = 2 * HEAD_DIM
    weight_pair = jnp.concatenate([w_key, w_value], axis=1)
    noisy_bundle = jnp.concatenate([queries[0, 1], grad_out[0, 1]], axis=1)
    weight_row, noisy_bundle = lax.optimization_barrier(
        (gather_z(weight_pair), turned_over(noisy_bundle, "context_0"))
    )
    noisy_bundle = turned_over(noisy_bundle, "context_1")
    weight_pieces = gather_ring(weight_row, "context_0")
    mine = tokens[0].reshape(2 * shard_rows, features)
    other = swapped(mine)
    width = queries.shape[3]
    full_tokens = jnp.concatenate(
        [jnp.where(head == 0, mine, other), jnp.where(head == 0, other, mine)], axis=1
    )
    weights = in_place_order(weight_pieces, row_y)
    projected, noisy_bundle = lax.optimization_barrier(
        (dot(full_tokens, weights).astype(BF16), noisy_bundle)
    )
    kv_pieces = gather_ring(gather_z(projected[:shard_rows]), "context_0")
    kv_noisy = mirrored(projected[shard_rows:])
    block_size = block_len[0]
    shift = 3 + (block_size > 8).astype(jnp.int32) + (block_size > 16).astype(jnp.int32)
    info = jnp.stack([row_y, my_index, size - 1 - my_index, shift]).astype(jnp.int32)
    dq_clean, dq_noisy, *pair_pieces, pair_noisy = attention(
        info,
        queries[0, 0],
        grad_out[0, 0],
        noisy_bundle[:, :width],
        noisy_bundle[:, width:],
        kv_pieces,
        kv_noisy,
    )
    returned = jnp.concatenate([dq_noisy, pair_noisy], axis=1)
    returned = turned_over(returned, "context_1")
    pair_row, returned = lax.optimization_barrier(
        (reduce_ring(pair_pieces, "context_0").astype(BF16), returned)
    )
    pair_clean, returned = lax.optimization_barrier(
        (scatter_z(pair_row).astype(BF16), turned_over(returned, "context_0"))
    )
    dq_noisy, pair_noisy = returned[:, :width], returned[:, width:]
    pair_grads = jnp.concatenate([pair_clean, pair_noisy], axis=0)

    weight_local = lax.dot_general(
        full_tokens, pair_grads, (((0,), (0,)), ((), ())), preferred_element_type=F32
    ).astype(BF16)
    quarter = weight_local.shape[0] // 4
    half = quarter // 2

    def part_of(step):
        return lax.dynamic_slice_in_dim(weight_local, ((row_y - step) & 3) * quarter, quarter, 0)

    far = part_of(2)
    weight_sum = scatter_z(
        reduce_ring(
            (part_of(0), part_of(1), far[:half], far[half:], part_of(3)), "context_0"
        ).astype(BF16)
    ).astype(BF16)
    copies = jnp.broadcast_to(weight_sum, (lax.axis_size("dp"), *weight_sum.shape))
    weight_sum = jnp.sum(lax.all_to_all(copies, "dp", 0, 0, tiled=True).astype(F32), axis=0)

    terms = lax.dot_general(
        pair_grads, weights, (((1,), (1,)), ((), ())), preferred_element_type=F32
    ).astype(BF16)
    low, high = terms[:, :features], terms[:, features:]
    kept = jnp.where(head == 0, low, high)
    given = swapped(jnp.where(head == 0, high, low))
    grad_x = (kept.astype(F32) + given.astype(F32)).astype(BF16).reshape(tokens.shape)
    grad_query = jnp.stack([dq_clean, dq_noisy])[None]
    return (grad_query, grad_x, weight_sum[:, :HEAD_DIM], weight_sum[:, HEAD_DIM:])


def solution(mesh):
    torus = Mesh(
        mesh.devices.reshape(mesh.shape["dp"], 4, 8, mesh.shape["head"]),
        ("dp", "context_0", "context_1", "head"),
    )
    in_specs = (
        P("dp", None, CONTEXT, "head"),
        P("dp", None, CONTEXT, "head"),
        P("dp", None, CONTEXT, "head"),
        P(CONTEXT, "head"),
        P(CONTEXT, "head"),
        P("dp"),
    )
    out_specs = (
        P("dp", None, CONTEXT, "head"),
        P("dp", None, CONTEXT, "head"),
        P(CONTEXT, "head"),
        P(CONTEXT, "head"),
    )
    return jax.shard_map(
        per_device, mesh=torus, in_specs=in_specs, out_specs=out_specs, check_vma=False
    )
```

time: 511 us -> 228 us (0.45)
  waiting for transfers between devices: 362 us -> 87.4 us
  starting transfers between devices: 9.64 us -> 65.4 us
  matrix products: 37.9 us -> 4.95 us
  Pallas kernels: 0 us -> 23.1 us
  local copies, waits for them, and re-layouts: 30.2 us -> 7.57 us
  other arithmetic: 33.4 us -> 14.9 us
  between operations: 15.2 us -> 1.72 us
    reduce_scatter x3 -> x0, waiting for transfers between devices: 220 us -> none  [the longest x1 162 us: summed_rows(): array = lax.psum_scatter(array, axis, scatter_dimension=dim, tiled=True)]
    all_gather x2 -> x0, waiting for transfers between devices: 74.1 us -> none  [the longest x1 70.5 us: per_device(): lax.all_gather(weight_pair, CONTEXT, axis=0, tiled=True)]
    ppermute x0 -> x23, waiting for transfers between devices: none -> 58.5 us  [the longest x16 44.6 us: shifted(): lax.ppermute(array, axis, [(i, (i + step) % size) for i in range(size)])]
    ppermute x0 -> x23, starting transfers between devices: none -> 42.4 us  [the longest x16 21.1 us: shifted(): lax.ppermute(array, axis, [(i, (i + step) % size) for i in range(size)])]
    dot_general x23 -> x3, matrix products: 37.9 us -> 4.95 us  [the longest x1 2.26 us: per_device(): lax.dot_general(pair_grads, weights, (((1,), (1,)), ((), ())), preferred_...]
    unnamed x7 -> x0, waiting for transfers between devices: 32.3 us -> none
    pallas_call x0 -> x1, Pallas kernels: none -> 23.1 us  [attention(): pl.pallas_call(attention_kernel, out_shape=(shape((rows, width), BF16), s...]
    all_to_all x2 -> x4, starting transfers between devices: 9.14 us -> 23 us  [the longest x2 9.82 us: scatter_z(): tiles = lax.all_to_all(tiles, 'context_1', 0, 0, tiled=True)]
  transfers between devices with their start and end apart: 8 -> 27, of which waited for: 8 -> 15; matrix products, arithmetic and copies ran while one was open for 12% -> 9% of each run, Pallas kernels for 0% -> 0%
where the time goes in v1:
time: 228 us; the launch traced here: 223 us
  waiting for transfers between devices  87.4 us (38%)
  starting transfers between devices  65.4 us (29%)
  Pallas kernels  23.1 us (10%)
  blocking collectives  18.3 us (8%)
  other arithmetic  14.9 us (7%)
  local copies, waits for them, and re-layouts  7.57 us (3%)
  matrix products  4.95 us (2%)
    ppermute x16, waiting for transfers between devices, shifted(): lax.ppermute(array, axis, [(i, (i + step) % size) for i in range(size)])  44.6 us
    pallas_call x1, Pallas kernels, attention(): pl.pallas_call(attention_kernel, out_shape=(shape((rows, width), BF16), s...  23.1 us
    all_to_all x2, waiting for transfers between devices, scatter_z(): tiles = lax.all_to_all(tiles, 'context_1', 0, 0, tiled=True)  23 us
    ppermute x16, starting transfers between devices, shifted(): lax.ppermute(array, axis, [(i, (i + step) % size) for i in range(size)])  21.1 us
    all_to_all x1, blocking collectives, gather_z(): tiles = lax.all_to_all(copies, 'context_1', 0, 0, tiled=True)  18.3 us
    ppermute x2, starting transfers between devices, swapped(): return lax.ppermute(array, 'head', [(0, 1), (1, 0)])  16.2 us
    ppermute x4, waiting for transfers between devices, turned_over(): return lax.ppermute(array, axis, [(i, size - 1 - i) for i in range(size)])  13.9 us
    all_to_all x2, starting transfers between devices, scatter_z(): tiles = lax.all_to_all(tiles, 'context_1', 0, 0, tiled=True)  9.82 us
  transfers between devices with their start and end apart: 27, of which 15 were waited for; matrix products, arithmetic and copies ran while one was open for 9% of the time, Pallas kernels for 0%

profile of v1, /device:TPU:1, one launch (start us, length us, event | category | flops | bytes accessed | tf_op | source)
XLA Modules:
  0.0 223.3 jit_solution(13431349912456882772)
XLA Ops:
  2.4 9.1 %all-to-all-start = ((bf16[8,128,256]{2,1,0:T(8,128)(2,1)}), bf16[8,128,256]{2,1,0:T(8,128)(2,1)S(1)}, u32[]{:S(2)}, u32[]{:S(2)}) async-start(bf16[8,128,256]{2,1,0:T(8,128)(2,1)} %broadcast_in_dim.12), calls=%async_computation | async-start | bytes 1048576 | tf_op jit(solution)/shard_map/all_to_all | solution.py:47
  12.4 2.8 %collective-permute-start.1 = (bf16[128,2048]{1,0:T(8,128)(2,1)S(1)}, bf16[128,2048]{1,0:T(8,128)(2,1)}, u32[]{:S(2)}, u32[]{:S(2)}) collective-permute-start(bf16[128,2048]{1,0:T(8,128)(2,1)S(1)} %pad_maximum_fusion.7), channel_id=1, source_target_pairs={{0,48},{16,32},{32,16},{48,0},{1,49},{17,33},{33,17},{49,1},{2,50}... | collective-permute-start | bytes 1572872 | tf_op jit(solution)/shard_map/ppermute | solution.py:38
  16.5 9.9 %collective-permute-done.1 = bf16[128,2048]{1,0:T(8,128)(2,1)} collective-permute-done((bf16[128,2048]{1,0:T(8,128)(2,1)S(1)}, bf16[128,2048]{1,0:T(8,128)(2,1)}, u32[]{:S(2)}, u32[]{:S(2)}) %collective-permute-start.1) | collective-permute-done | bytes 524320 | tf_op jit(solution)/shard_map/ppermute | solution.py:38
  26.4 3.0 %all-to-all-done = bf16[8,128,256]{2,1,0:T(8,128)(2,1)S(1)} async-done(((bf16[8,128,256]{2,1,0:T(8,128)(2,1)}), bf16[8,128,256]{2,1,0:T(8,128)(2,1)S(1)}, u32[]{:S(2)}, u32[]{:S(2)}) %all-to-all-start) | async-done | bytes 524320 | tf_op jit(solution)/shard_map/all_to_all | solution.py:47
  32.2 11.6 %collective-permute-done.2 = bf16[1024,256]{1,0:T(8,128)(2,1)S(1)} collective-permute-done((bf16[1024,256]{1,0:T(8,128)(2,1)S(1)}, bf16[1024,256]{1,0:T(8,128)(2,1)S(1)}, u32[]{:S(2)}, u32[]{:S(2)}) %collective-permute-start.2) | collective-permute-done | bytes 524320 | tf_op jit(solution)/shard_map/ppermute | solution.py:28
  43.9 2.7 %collective-permute-start.5 = (bf16[512,256]{1,0:T(8,128)(2,1)S(1)}, bf16[512,256]{1,0:T(8,128)(2,1)S(1)}, u32[]{:S(2)}, u32[]{:S(2)}) collective-permute-start(bf16[512,256]{1,0:T(8,128)(2,1)S(1)} %slice.113), channel_id=1, source_target_pairs={{0,48},{16,0},{32,16},{48,32},{1,49},{17,1},{33,17},{49,33},{2,50}... | collective-permute-start | bytes 786440 | tf_op jit(solution)/shard_map/ppermute | solution.py:28
  48.1 3.6 %collective-permute-done.3 = bf16[512,256]{1,0:T(8,128)(2,1)S(1)} collective-permute-done((bf16[512,256]{1,0:T(8,128)(2,1)S(1)}, bf16[512,256]{1,0:T(8,128)(2,1)S(1)}, u32[]{:S(2)}, u32[]{:S(2)}) %collective-permute-start.3) | collective-permute-done | bytes 262176 | tf_op jit(solution)/shard_map/ppermute | solution.py:28
  53.4 3.9 %collective-permute-done.6 = bf16[128,2048]{1,0:T(8,128)(2,1)S(1)} collective-permute-done((bf16[128,2048]{1,0:T(8,128)(2,1)}, bf16[128,2048]{1,0:T(8,128)(2,1)S(1)}, u32[]{:S(2)}, u32[]{:S(2)}) %collective-permute-start.6) | collective-permute-done | bytes 524320 | tf_op jit(solution)/shard_map/ppermute | solution.py:38
  57.4 18.3 %all_to_all.25 = bf16[8,128,256]{2,1,0:T(8,128)(2,1)S(1)} all-to-all(bf16[8,128,256]{2,1,0:T(8,128)(2,1)S(1)} %broadcast_in_dim.13), channel_id=1, replica_groups=mesh['dp'=4,'context_0'=4,'context_1'=8,'head'=2] {'context_1'}, dimensions={0} | all-to-all | bytes 1048576 | tf_op jit(solution)/shard_map/all_to_all | solution.py:47
  77.8 7.7 %collective-permute-done.9.kv_3 = bf16[1024,256]{1,0:T(8,128)(2,1)S(1)} collective-permute-done((bf16[1024,256]{1,0:T(8,128)(2,1)S(1)}, bf16[1024,256]{1,0:T(8,128)(2,1)S(1)}, u32[]{:S(2)}, u32[]{:S(2)}) %collective-permute-start.9) | collective-permute-done | bytes 524320 | tf_op jit(solution)/shard_map/ppermute | solution.py:28
  96.3 23.1 %shard_map.93 = (bf16[128,1024]{1,0:T(8,128)(2,1)}, bf16[128,1024]{1,0:T(8,128)(2,1)}, bf16[1024,256]{1,0:T(8,128)(2,1)}, bf16[1024,256]{1,0:T(8,128)(2,1)}, bf1...) custom-call(s32[4]{0:T(128)} %pad_add_fusion.info, ...), custom_call_target="tpu_custom_call" | custom-call | tf_op jit(solution)/shard_map/pallas_call | solution.py:280
  120.5 2.7 %collective-permute-start.14 = (bf16[512,256]{1,0:T(8,128)(2,1)}, bf16[512,256]{1,0:T(8,128)(2,1)S(1)}, u32[]{:S(2)}, u32[]{:S(2)}) collective-permute-start(bf16[512,256]{1,0:T(8,128)(2,1)} %get-tuple-element.29), channel_id=1, source_target_pairs={{0,48},{16,0},{32,16},{48,32},{1,49},{17,1},{33,17},{49,33},{2,50}... | collective-permute-start | bytes 786440 | tf_op jit(solution)/shard_map/ppermute | solution.py:28
  127.4 2.7 %collective-permute-start.15 = (bf16[1024,256]{1,0:T(8,128)(2,1)S(1)}, bf16[1024,256]{1,0:T(8,128)(2,1)S(1)}, u32[]{:S(2)}, u32[]{:S(2)}) collective-permute-start(bf16[1024,256]{1,0:T(8,128)(2,1)S(1)} %pad_maximum_fusion.10), channel_id=1, source_target_pairs={{0,48},{16,0},{32,16},{48,32},{1,49},{17,1},{33,17},{49,33},{2,50}... | collective-permute-start | bytes 1572872 | tf_op jit(solution)/shard_map/ppermute | solution.py:28
  130.3 7.9 %collective-permute-done.13 = bf16[1024,256]{1,0:T(8,128)(2,1)S(1)} collective-permute-done((bf16[1024,256]{1,0:T(8,128)(2,1)S(1)}, bf16[1024,256]{1,0:T(8,128)(2,1)S(1)}, u32[]{:S(2)}, u32[]{:S(2)}) %collective-permute-start.13) | collective-permute-done | bytes 524320 | tf_op jit(solution)/shard_map/ppermute | solution.py:28
  140.0 6.3 %all-to-all-start.2 = ((bf16[8,128,256]{2,1,0:T(8,128)(2,1)}), bf16[8,128,256]{2,1,0:T(8,128)(2,1)S(1)}, u32[]{:S(2)}, u32[]{:S(2)}) async-start(bf16[8,128,256]{2,1,0:T(8,128)(2,1)} %bitcast.19), calls=%async_computation.2 | async-start | bytes 1048576 | tf_op jit(solution)/shard_map/all_to_all | solution.py:79
  148.4 10.1 %all-to-all-done.2 = bf16[8,128,256]{2,1,0:T(8,128)(2,1)S(1)} async-done(((bf16[8,128,256]{2,1,0:T(8,128)(2,1)}), bf16[8,128,256]{2,1,0:T(8,128)(2,1)S(1)}, u32[]{:S(2)}, u32[]{:S(2)}) %all-to-all-start.2) | async-done | bytes 524320 | tf_op jit(solution)/shard_map/all_to_all | solution.py:79
  164.1 6.2 %collective-permute-done.19 = bf16[512,256]{1,0:T(8,128)(2,1)} collective-permute-done((bf16[512,256]{1,0:T(8,128)(2,1)S(1)}, bf16[512,256]{1,0:T(8,128)(2,1)}, u32[]{:S(2)}, u32[]{:S(2)}) %collective-permute-start.19) | collective-permute-done | bytes 262176 | tf_op jit(solution)/shard_map/ppermute | solution.py:28
  171.8 2.7 %collective-permute-start.22 = (bf16[1024,256]{1,0:T(8,128)(2,1)S(1)}, bf16[1024,256]{1,0:T(8,128)(2,1)S(1)}, u32[]{:S(2)}, u32[]{:S(2)}) collective-permute-start(bf16[1024,256]{1,0:T(8,128)(2,1)S(1)} %pad_maximum_fusion.12), channel_id=1, source_target_pairs={{0,48},{16,0},{32,16},{48,32},{1,49},{17,1},{33,17},{49,33},{2,50}... | collective-permute-start | bytes 1572872 | tf_op jit(solution)/shard_map/ppermute | solution.py:28
  177.9 14.9 %collective-permute-start.18 = (bf16[256,2048]{1,0:T(8,128)(2,1)}, bf16[256,2048]{1,0:T(8,128)(2,1)}, u32[]{:S(2)}, u32[]{:S(2)}) collective-permute-start(bf16[256,2048]{1,0:T(8,128)(2,1)} %broadcast_select_fusion), channel_id=1, source_target_pairs={{0,1},{1,0},{2,3},{3,2},{4,5},{5,4},{6,7},{7,6},{8,9},{9,8},{10,11... | collective-permute-start | bytes 3145736 | tf_op jit(solution)/shard_map/ppermute | solution.py:42
  194.9 3.5 %all-to-all-start.3 = ((bf16[8,128,256]{2,1,0:T(8,128)(2,1)}), bf16[8,128,256]{2,1,0:T(8,128)(2,1)S(1)}, u32[]{:S(2)}, u32[]{:S(2)}) async-start(bf16[8,128,256]{2,1,0:T(8,128)(2,1)} %bitcast.23), calls=%async_computation.3 | async-start | bytes 1048576 | tf_op jit(solution)/shard_map/all_to_all | solution.py:79
  199.2 13.0 %all-to-all-done.3 = bf16[8,128,256]{2,1,0:T(8,128)(2,1)S(1)} async-done(((bf16[8,128,256]{2,1,0:T(8,128)(2,1)}), bf16[8,128,256]{2,1,0:T(8,128)(2,1)S(1)}, u32[]{:S(2)}, u32[]{:S(2)}) %all-to-all-start.3) | async-done | bytes 524320 | tf_op jit(solution)/shard_map/all_to_all | solution.py:79
  213.0 4.0 %all-to-all-start.4 = ((bf16[4,128,256]{2,1,0:T(8,128)(2,1)}), bf16[4,128,256]{2,1,0:T(8,128)(2,1)S(1)}, u32[]{:S(2)}, u32[]{:S(2)}) async-start(bf16[4,128,256]{2,1,0:T(8,128)(2,1)} %broadcast_in_dim.15), calls=%async_computation.4 | async-start | bytes 524288 | tf_op jit(solution)/shard_map/all_to_all | solution.py:391
  217.0 2.7 %add_convert_fusion = bf16[256,2048]{1,0:T(8,128)(2,1)} fusion(bf16[256,2048]{1,0:T(8,128)(2,1)} %collective-permute-done.18, pred[]{:T(512)S(6)} %eq.2, bf16[256,4096]{1,0:T(8,128)(2,1)S(1)} %convolution_convert_fusion.1), kind=kLoop, calls=%fused_computation.5 | loop fusion | flops 2621440 | bytes 4194305 | tf_op jit(solution)/shard_map/convert_element_type | solution.py:399
  219.7 2.8 %all-to-all-done.4 = bf16[4,128,256]{2,1,0:T(8,128)(2,1)S(1)} async-done(((bf16[4,128,256]{2,1,0:T(8,128)(2,1)}), bf16[4,128,256]{2,1,0:T(8,128)(2,1)S(1)}, u32[]{:S(2)}, u32[]{:S(2)}) %all-to-all-start.4) | async-done | bytes 262176 | tf_op jit(solution)/shard_map/all_to_all | solution.py:391
  (117 shorter events, 46.2 us)
Async XLA Ops:
  2.4 27.1 %all-to-all-start = ((bf16[8,128,256]{2,1,0:T(8,128)(2,1)}), bf16[8,128,256]{2,1,0:T(8,128)(2,1)S(1)}, u32[]{:S(2)}, u32[]{:S(2)}) async-start(bf16[8,128,256]{2,1,0:T(8,128)(2,1)} %broadcast_in_dim.12), calls=%async_computation | async-start | bytes 1048576 | tf_op jit(solution)/shard_map/all_to_all | solution.py:47
  12.4 14.0 %collective-permute-start.1 = (bf16[128,2048]{1,0:T(8,128)(2,1)S(1)}, bf16[128,2048]{1,0:T(8,128)(2,1)}, u32[]{:S(2)}, u32[]{:S(2)}) collective-permute-start(bf16[128,2048]{1,0:T(8,128)(2,1)S(1)} %pad_maximum_fusion.7), channel_id=1, source_target_pairs={{0,48},{16,32},{32,16},{48,0},{1,49},{17,33},{33,17},{49,1},{2,50}... | collective-permute-start | bytes 1572872 | tf_op jit(solution)/shard_map/ppermute | solution.py:38
  15.2 31.5 %collective-permute-start = (bf16[256,2048]{1,0:T(8,128)(2,1)S(1)}, bf16[256,2048]{1,0:T(8,128)(2,1)}, u32[]{:S(2)}, u32[]{:S(2)}) collective-permute-start(bf16[256,2048]{1,0:T(8,128)(2,1)S(1)} %bitcast.45), channel_id=1, source_target_pairs={{0,1},{1,0},{2,3},{3,2},{4,5},{5,4},{6,7},{7,6},{8,9},{9,8},{10,11... | collective-permute-start | bytes 3145736 | tf_op jit(solution)/shard_map/ppermute | solution.py:42
  29.5 14.3 %collective-permute-start.2 = (bf16[1024,256]{1,0:T(8,128)(2,1)S(1)}, bf16[1024,256]{1,0:T(8,128)(2,1)S(1)}, u32[]{:S(2)}, u32[]{:S(2)}) collective-permute-start(bf16[1024,256]{1,0:T(8,128)(2,1)S(1)} %bitcast.40), channel_id=1, source_target_pairs={{0,16},{16,32},{32,48},{48,0},{1,17},{17,33},{33,49},{49,1},{2,18}... | collective-permute-start | bytes 1572872 | tf_op jit(solution)/shard_map/ppermute | solution.py:28
  30.8 13.2 %collective-permute-start.4 = (bf16[1024,256]{1,0:T(8,128)(2,1)S(1)}, bf16[1024,256]{1,0:T(8,128)(2,1)S(1)}, u32[]{:S(2)}, u32[]{:S(2)}) collective-permute-start(bf16[1024,256]{1,0:T(8,128)(2,1)S(1)} %bitcast.41), channel_id=1, source_target_pairs={{0,48},{16,0},{32,16},{48,32},{1,49},{17,1},{33,17},{49,33},{2,50}... | collective-permute-start | bytes 1572872 | tf_op jit(solution)/shard_map/ppermute | solution.py:28
  32.2 25.2 %collective-permute-start.6 = (bf16[128,2048]{1,0:T(8,128)(2,1)}, bf16[128,2048]{1,0:T(8,128)(2,1)S(1)}, u32[]{:S(2)}, u32[]{:S(2)}) collective-permute-start(bf16[128,2048]{1,0:T(8,128)(2,1)} %collective-permute-done.1), channel_id=1, source_target_pairs={{0,14},{2,12},{4,10},{6,8},{8,6},{10,4},{12,2},{14,0},{1,15},{3,13... | collective-permute-start | bytes 1572872 | tf_op jit(solution)/shard_map/ppermute | solution.py:38
  43.8 7.8 %collective-permute-start.3 = (bf16[512,256]{1,0:T(8,128)(2,1)S(1)}, bf16[512,256]{1,0:T(8,128)(2,1)S(1)}, u32[]{:S(2)}, u32[]{:S(2)}) collective-permute-start(bf16[512,256]{1,0:T(8,128)(2,1)S(1)} %slice.112), channel_id=1, source_target_pairs={{0,16},{16,32},{32,48},{48,0},{1,17},{17,33},{33,49},{49,1},{2,18}... | collective-permute-start | bytes 786440 | tf_op jit(solution)/shard_map/ppermute | solution.py:28
  43.9 7.7 %collective-permute-start.5 = (bf16[512,256]{1,0:T(8,128)(2,1)S(1)}, bf16[512,256]{1,0:T(8,128)(2,1)S(1)}, u32[]{:S(2)}, u32[]{:S(2)}) collective-permute-start(bf16[512,256]{1,0:T(8,128)(2,1)S(1)} %slice.113), channel_id=1, source_target_pairs={{0,48},{16,0},{32,16},{48,32},{1,49},{17,1},{33,17},{49,33},{2,50}... | collective-permute-start | bytes 786440 | tf_op jit(solution)/shard_map/ppermute | solution.py:28
  75.7 9.8 %collective-permute-start.9 = (bf16[1024,256]{1,0:T(8,128)(2,1)S(1)}, bf16[1024,256]{1,0:T(8,128)(2,1)S(1)}, u32[]{:S(2)}, u32[]{:S(2)}) collective-permute-start(bf16[1024,256]{1,0:T(8,128)(2,1)S(1)} %bitcast.37), channel_id=1, source_target_pairs={{0,48},{16,0},{32,16},{48,32},{1,49},{17,1},{33,17},{49,33},{2,50}... | collective-permute-start | bytes 1572872 | tf_op jit(solution)/shard_map/ppermute | solution.py:28
  77.1 11.2 %collective-permute-start.7 = (bf16[1024,256]{1,0:T(8,128)(2,1)S(1)}, bf16[1024,256]{1,0:T(8,128)(2,1)S(1)}, u32[]{:S(2)}, u32[]{:S(2)}) collective-permute-start(bf16[1024,256]{1,0:T(8,128)(2,1)S(1)} %bitcast.38), channel_id=1, source_target_pairs={{0,16},{16,32},{32,48},{48,0},{1,17},{17,33},{33,49},{49,1},{2,18}... | collective-permute-start | bytes 1572872 | tf_op jit(solution)/shard_map/ppermute | solution.py:28
  119.4 6.7 %collective-permute-start.12 = (bf16[512,256]{1,0:T(8,128)(2,1)}, bf16[512,256]{1,0:T(8,128)(2,1)S(1)}, u32[]{:S(2)}, u32[]{:S(2)}) collective-permute-start(bf16[512,256]{1,0:T(8,128)(2,1)} %get-tuple-element.27), channel_id=1, source_target_pairs={{0,16},{16,32},{32,48},{48,0},{1,17},{17,33},{33,49},{49,1},{2,18}... | collective-permute-start | bytes 786440 | tf_op jit(solution)/shard_map/ppermute | solution.py:28
  120.5 6.8 %collective-permute-start.14 = (bf16[512,256]{1,0:T(8,128)(2,1)}, bf16[512,256]{1,0:T(8,128)(2,1)S(1)}, u32[]{:S(2)}, u32[]{:S(2)}) collective-permute-start(bf16[512,256]{1,0:T(8,128)(2,1)} %get-tuple-element.29), channel_id=1, source_target_pairs={{0,48},{16,0},{32,16},{48,32},{1,49},{17,1},{33,17},{49,33},{2,50}... | collective-permute-start | bytes 786440 | tf_op jit(solution)/shard_map/ppermute | solution.py:28
  127.1 11.1 %collective-permute-start.13 = (bf16[1024,256]{1,0:T(8,128)(2,1)S(1)}, bf16[1024,256]{1,0:T(8,128)(2,1)S(1)}, u32[]{:S(2)}, u32[]{:S(2)}) collective-permute-start(bf16[1024,256]{1,0:T(8,128)(2,1)S(1)} %pad_maximum_fusion.9), channel_id=1, source_target_pairs={{0,16},{16,32},{32,48},{48,0},{1,17},{17,33},{33,49},{49,1},{2,18}... | collective-permute-start | bytes 1572872 | tf_op jit(solution)/shard_map/ppermute | solution.py:28
  127.4 11.7 %collective-permute-start.15 = (bf16[1024,256]{1,0:T(8,128)(2,1)S(1)}, bf16[1024,256]{1,0:T(8,128)(2,1)S(1)}, u32[]{:S(2)}, u32[]{:S(2)}) collective-permute-start(bf16[1024,256]{1,0:T(8,128)(2,1)S(1)} %pad_maximum_fusion.10), channel_id=1, source_target_pairs={{0,48},{16,0},{32,16},{48,32},{1,49},{17,1},{33,17},{49,33},{2,50}... | collective-permute-start | bytes 1572872 | tf_op jit(solution)/shard_map/ppermute | solution.py:28
  130.1 9.9 %collective-permute-start.16 = (bf16[128,1280]{1,0:T(8,128)(2,1)S(1)}, bf16[128,1280]{1,0:T(8,128)(2,1)S(1)}, u32[]{:S(2)}, u32[]{:S(2)}) collective-permute-start(bf16[128,1280]{1,0:T(8,128)(2,1)S(1)} %pad_maximum_fusion.15), channel_id=1, source_target_pairs={{0,14},{2,12},{4,10},{6,8},{8,6},{10,4},{12,2},{14,0},{1,15},{3,13... | collective-permute-start | bytes 983048 | tf_op jit(solution)/shard_map/ppermute | solution.py:38
  140.0 18.5 %all-to-all-start.2 = ((bf16[8,128,256]{2,1,0:T(8,128)(2,1)}), bf16[8,128,256]{2,1,0:T(8,128)(2,1)S(1)}, u32[]{:S(2)}, u32[]{:S(2)}) async-start(bf16[8,128,256]{2,1,0:T(8,128)(2,1)} %bitcast.19), calls=%async_computation.2 | async-start | bytes 1048576 | tf_op jit(solution)/shard_map/all_to_all | solution.py:79
  146.3 12.8 %collective-permute-start.17 = (bf16[128,1280]{1,0:T(8,128)(2,1)S(1)}, bf16[128,1280]{1,0:T(8,128)(2,1)S(1)}, u32[]{:S(2)}, u32[]{:S(2)}) collective-permute-start(bf16[128,1280]{1,0:T(8,128)(2,1)S(1)} %collective-permute-done.16), channel_id=1, source_target_pairs={{0,48},{16,32},{32,16},{48,0},{1,49},{17,33},{33,17},{49,1},{2,50}... | collective-permute-start | bytes 983048 | tf_op jit(solution)/shard_map/ppermute | solution.py:38
  161.3 8.9 %collective-permute-start.19 = (bf16[512,256]{1,0:T(8,128)(2,1)S(1)}, bf16[512,256]{1,0:T(8,128)(2,1)}, u32[]{:S(2)}, u32[]{:S(2)}) collective-permute-start(bf16[512,256]{1,0:T(8,128)(2,1)S(1)} %get-tuple-element.38), channel_id=1, source_target_pairs={{0,16},{16,32},{32,48},{48,0},{1,17},{17,33},{33,49},{49,1},{2,18}... | collective-permute-start | bytes 786440 | tf_op jit(solution)/shard_map/ppermute | solution.py:28
  161.4 8.9 %collective-permute-start.21 = (bf16[512,256]{1,0:T(8,128)(2,1)S(1)}, bf16[512,256]{1,0:T(8,128)(2,1)}, u32[]{:S(2)}, u32[]{:S(2)}) collective-permute-start(bf16[512,256]{1,0:T(8,128)(2,1)S(1)} %get-tuple-element.40), channel_id=1, source_target_pairs={{0,48},{16,0},{32,16},{48,32},{1,49},{17,1},{33,17},{49,33},{2,50}... | collective-permute-start | bytes 786440 | tf_op jit(solution)/shard_map/ppermute | solution.py:28
  171.5 21.4 %collective-permute-start.20 = (bf16[1024,256]{1,0:T(8,128)(2,1)S(1)}, bf16[1024,256]{1,0:T(8,128)(2,1)S(1)}, u32[]{:S(2)}, u32[]{:S(2)}) collective-permute-start(bf16[1024,256]{1,0:T(8,128)(2,1)S(1)} %pad_maximum_fusion.11), channel_id=1, source_target_pairs={{0,16},{16,32},{32,48},{48,0},{1,17},{17,33},{33,49},{49,1},{2,18}... | collective-permute-start | bytes 1572872 | tf_op jit(solution)/shard_map/ppermute | solution.py:28
  171.8 21.0 %collective-permute-start.22 = (bf16[1024,256]{1,0:T(8,128)(2,1)S(1)}, bf16[1024,256]{1,0:T(8,128)(2,1)S(1)}, u32[]{:S(2)}, u32[]{:S(2)}) collective-permute-start(bf16[1024,256]{1,0:T(8,128)(2,1)S(1)} %pad_maximum_fusion.12), channel_id=1, source_target_pairs={{0,48},{16,0},{32,16},{48,32},{1,49},{17,1},{33,17},{49,33},{2,50}... | collective-permute-start | bytes 1572872 | tf_op jit(solution)/shard_map/ppermute | solution.py:28
  177.9 39.1 %collective-permute-start.18 = (bf16[256,2048]{1,0:T(8,128)(2,1)}, bf16[256,2048]{1,0:T(8,128)(2,1)}, u32[]{:S(2)}, u32[]{:S(2)}) collective-permute-start(bf16[256,2048]{1,0:T(8,128)(2,1)} %broadcast_select_fusion), channel_id=1, source_target_pairs={{0,1},{1,0},{2,3},{3,2},{4,5},{5,4},{6,7},{7,6},{8,9},{9,8},{10,11... | collective-permute-start | bytes 3145736 | tf_op jit(solution)/shard_map/ppermute | solution.py:42
  194.9 17.4 %all-to-all-start.3 = ((bf16[8,128,256]{2,1,0:T(8,128)(2,1)}), bf16[8,128,256]{2,1,0:T(8,128)(2,1)S(1)}, u32[]{:S(2)}, u32[]{:S(2)}) async-start(bf16[8,128,256]{2,1,0:T(8,128)(2,1)} %bitcast.23), calls=%async_computation.3 | async-start | bytes 1048576 | tf_op jit(solution)/shard_map/all_to_all | solution.py:79
  213.0 9.5 %all-to-all-start.4 = ((bf16[4,128,256]{2,1,0:T(8,128)(2,1)}), bf16[4,128,256]{2,1,0:T(8,128)(2,1)S(1)}, u32[]{:S(2)}, u32[]{:S(2)}) async-start(bf16[4,128,256]{2,1,0:T(8,128)(2,1)} %broadcast_in_dim.15), calls=%async_computation.4 | async-start | bytes 524288 | tf_op jit(solution)/shard_map/all_to_all | solution.py:391
  (24 other events, 211.9 us)

commit v2 on v1

v2 whole, which is shorter than its diff:
```python
import math

import jax
import jax.numpy as jnp
from jax import lax
from jax.experimental import pallas as pl
from jax.experimental.pallas import tpu as pltpu
from jax.sharding import Mesh
from jax.sharding import PartitionSpec as P

HEAD_DIM = 128
CONTEXT = ("context_0", "context_1")
BF16 = jnp.bfloat16
F32 = jnp.float32
MASKED = -1e30
SCALE = 1.0 / math.sqrt(HEAD_DIM)
EXP_SCALE = math.log2(math.e) / math.sqrt(HEAD_DIM)
BLOCK = 256
LANES = 256
CHUNKS = 8 * HEAD_DIM // LANES
PER_CHUNK = LANES // HEAD_DIM


def dot(left, right):
    return jnp.dot(left, right, preferred_element_type=F32)


def shifted(array, axis, step):
    size = lax.axis_size(axis)
    return lax.ppermute(array, axis, [(i, (i + step) % size) for i in range(size)])


def turned_over(array, axis):
    size = lax.axis_size(axis)
    return lax.ppermute(array, axis, [(i, size - 1 - i) for i in range(size)])


def swapped(array):
    return lax.ppermute(array, "head", [(0, 1), (1, 0)])


def gather_z(array):
    copies = jnp.broadcast_to(array, (lax.axis_size("context_1"), *array.shape))
    tiles = lax.all_to_all(copies, "context_1", 0, 0, tiled=True)
    return tiles.reshape(-1, *array.shape[1:])


def gather_ring(array, axis):
    half = array.shape[0] // 2
    before = shifted(array, axis, 1)
    after = shifted(array, axis, -1)
    far_low = shifted(before[:half], axis, 1)
    far_high = shifted(after[half:], axis, -1)
    return array, before, far_low, far_high, after


def reduce_ring(pieces, axis):
    own, before, far_low, far_high, after = pieces
    half = far_low.shape[0]
    got_low = shifted(far_low, axis, 1).astype(F32)
    got_high = shifted(far_high, axis, -1).astype(F32)
    up = after.astype(F32) + jnp.pad(got_low, ((0, half), (0, 0)))
    down = before.astype(F32) + jnp.pad(got_high, ((half, 0), (0, 0)))
    from_before = shifted(up.astype(BF16), axis, 1)
    from_after = shifted(down.astype(BF16), axis, -1)
    return own.astype(F32) + from_before.astype(F32) + from_after.astype(F32)


def scatter_z(array):
    size = lax.axis_size("context_1")
    tiles = array.reshape(size, array.shape[0] // size, array.shape[1])
    tiles = lax.all_to_all(tiles, "context_1", 0, 0, tiled=True)
    return jnp.sum(tiles.astype(F32), axis=0)


def attention_kernel(
    info,
    q_clean,
    g_clean,
    noisy,
    kv_0,
    kv_1,
    kv_2a,
    kv_2b,
    kv_3,
    dq_clean,
    out_noisy,
    out_0,
    out_1,
    out_2a,
    out_2b,
    out_3,
    kvs,
    qh,
    gh,
    qt,
    gt,
    weights,
    gprobs,
    weights_own,
    gprobs_own,
    peak,
    total,
    moment,
    used,
    used_own,
    dqt,
    acc,
):
    row_y = info[0]
    tile_clean = info[1]
    tile_noisy = info[2]
    shift = info[3]
    blocks_y = 4
    full_clean = tile_clean >> 1
    full_noisy = tile_noisy >> 1
    width = q_clean.shape[1]
    for part, sources in enumerate(((kv_0,), (kv_1,), (kv_2a, kv_2b), (kv_3,))):
        place = ((row_y - part) & 3) * blocks_y
        each = blocks_y // len(sources)
        for b in range(blocks_y):
            at = (b % each) * BLOCK
            kvs[place + b] = sources[b // each][at : at + BLOCK, :]
    for stream, (q_ref, g_ref, start) in enumerate(
        ((q_clean, g_clean, 0), (noisy, noisy, width))
    ):
        for h in range(PER_CHUNK * CHUNKS):
            at = slice((h % PER_CHUNK) * HEAD_DIM, (h % PER_CHUNK + 1) * HEAD_DIM)
            for ref, first, rows, turned in ((q_ref, 0, qh, qt), (g_ref, start, gh, gt)):
                first = first + h * HEAD_DIM
                tile = ref[:, first : first + HEAD_DIM]
                rows[stream, h // PER_CHUNK, at, :] = tile
                turned[stream, h // PER_CHUNK, :, at] = tile.T
    acc[...] = jnp.zeros_like(acc)

    lane = lax.broadcasted_iota(jnp.int32, (1, LANES), 1) & (HEAD_DIM - 1)

    def limits(tile, after):
        pos = tile * HEAD_DIM + lane
        return ((pos >> shift) + after) << shift

    def step_forward(stream, k, v, j, visible, first, save_w, save_g, save_used):
        s = dot(k, qt[stream, j])
        d = dot(v, gt[stream, j])
        if visible is not None:
            s = jnp.where(visible, s, MASKED)
        top = jnp.max(s, axis=0, keepdims=True)
        if first:
            new_peak = top
        else:
            old_peak = peak[stream, j]
            new_peak = jnp.maximum(old_peak, top)
            shrink = jnp.exp2((old_peak - new_peak) * EXP_SCALE)
        w = jnp.exp2((s - new_peak) * EXP_SCALE)
        sum_w = jnp.sum(w, axis=0, keepdims=True)
        sum_m = jnp.sum(w * d, axis=0, keepdims=True)
        if not first:
            sum_w = total[stream, j] * shrink + sum_w
            sum_m = moment[stream, j] * shrink + sum_m
        peak[stream, j] = new_peak
        total[stream, j] = sum_w
        moment[stream, j] = sum_m
        save_used(j, new_peak)
        save_w(j, w)
        save_g(j, d)

    def saver(ref, slot):
        def save(j, value):
            ref[slot, j] = value

        return save

    def forward_block(slot, stream, block, visible, first):
        k = kvs[block, :, :HEAD_DIM]
        v = kvs[block, :, HEAD_DIM:]
        for j in range(CHUNKS):
            step_forward(
                stream, k, v, j, visible, first,
                saver(weights, slot), saver(gprobs, slot), saver(used, slot),
            )

    def own_saver(ref):
        def save(j, value):
            ref[j] = value

        return save

    key_row = lax.broadcasted_iota(jnp.int32, (BLOCK, LANES), 0)
    own_row = lax.broadcasted_iota(jnp.int32, (HEAD_DIM, LANES), 0)
    same = (own_row >> shift) == (jnp.broadcast_to(lane, (HEAD_DIM, LANES)) >> shift)
    own_k = noisy[:, 2 * width : 2 * width + HEAD_DIM]
    own_v = noisy[:, 2 * width + HEAD_DIM :]
    for j in range(CHUNKS):
        step_forward(
            1, own_k, own_v, j, same, True,
            own_saver(weights_own), own_saver(gprobs_own), own_saver(used_own),
        )
    forward_block(18, 0, full_clean, key_row + full_clean * BLOCK < limits(tile_clean, 1), True)
    forward_block(19, 1, full_noisy, key_row + full_noisy * BLOCK < limits(tile_noisy, 0), False)

    def place_of(slot):
        clean = slot < full_clean
        return jnp.where(clean, 0, 1), jnp.where(clean, slot, slot - full_clean)

    def forward_turn(slot, carry):
        stream, block = place_of(slot)
        forward_block(slot, stream, block, None, False)
        return carry

    lax.fori_loop(0, full_clean + full_noisy, forward_turn, 0)

    for stream in range(2):
        for j in range(CHUNKS):
            inverse = 1.0 / total[stream, j]
            total[stream, j] = inverse
            moment[stream, j] = moment[stream, j] * inverse
            dqt[stream, j] = jnp.zeros((HEAD_DIM, LANES), F32)

    def step_backward(stream, kt, j, w, d, seen):
        factor = jnp.exp2((seen - peak[stream, j]) * EXP_SCALE) * total[stream, j]
        p = w * factor
        ds = (p * (d - moment[stream, j])).astype(BF16)
        dv = dot(p.astype(BF16), gh[stream, j])
        dk = dot(ds, qh[stream, j])
        dqt[stream, j] += dot(kt, ds)
        return dk, dv

    def backward_block(slot, stream, block):
        kt = kvs[block, :, :HEAD_DIM].T
        dk = jnp.zeros((BLOCK, HEAD_DIM), F32)
        dv = jnp.zeros((BLOCK, HEAD_DIM), F32)
        for j in range(CHUNKS):
            more_k, more_v = step_backward(
                stream, kt, j, weights[slot, j], gprobs[slot, j], used[slot, j]
            )
            dk += more_k
            dv += more_v
        acc[block, :, :HEAD_DIM] += dk * SCALE
        acc[block, :, HEAD_DIM:] += dv

    kt_own = own_k.T
    dk = jnp.zeros((HEAD_DIM, HEAD_DIM), F32)
    dv = jnp.zeros((HEAD_DIM, HEAD_DIM), F32)
    for j in range(CHUNKS):
        more_k, more_v = step_backward(1, kt_own, j, weights_own[j], gprobs_own[j], used_own[j])
        dk += more_k
        dv += more_v
    out_noisy[:, width : width + HEAD_DIM] = (dk * SCALE).astype(BF16)
    out_noisy[:, width + HEAD_DIM :] = dv.astype(BF16)

    def backward_turn(slot, carry):
        stream, block = place_of(slot)
        backward_block(slot, stream, block)
        return carry

    lax.fori_loop(0, full_clean + full_noisy, backward_turn, 0)
    backward_block(18, 0, full_clean)
    backward_block(19, 1, full_noisy)

    for stream, ref in enumerate((dq_clean, out_noisy)):
        for h in range(PER_CHUNK * CHUNKS):
            at = slice((h % PER_CHUNK) * HEAD_DIM, (h % PER_CHUNK + 1) * HEAD_DIM)
            tile = dqt[stream, h // PER_CHUNK, :, at]
            ref[:, h * HEAD_DIM : (h + 1) * HEAD_DIM] = (tile.T * SCALE).astype(BF16)
    for part, refs in enumerate(((out_0,), (out_1,), (out_2a, out_2b), (out_3,))):
        place = ((row_y - part) & 3) * blocks_y
        each = blocks_y // len(refs)
        for b in range(blocks_y):
            at = (b % each) * BLOCK
            refs[b // each][at : at + BLOCK, :] = acc[place + b].astype(BF16)


def attention(info, q_clean, g_clean, noisy, pieces):
    rows, width = q_clean.shape
    span, kv_width = pieces[0].shape
    vmem = pl.BlockSpec(memory_space=pltpu.VMEM)
    shape = jax.ShapeDtypeStruct
    slots = 20
    return pl.pallas_call(
        attention_kernel,
        out_shape=(
            shape((rows, width), BF16),
            shape((rows, width + kv_width), BF16),
            shape((span, kv_width), BF16),
            shape((span, kv_width), BF16),
            shape((span // 2, kv_width), BF16),
            shape((span // 2, kv_width), BF16),
            shape((span, kv_width), BF16),
        ),
        in_specs=[pl.BlockSpec(memory_space=pltpu.SMEM)] + [vmem] * 8,
        out_specs=(vmem,) * 7,
        scratch_shapes=[
            pltpu.VMEM((16, BLOCK, kv_width), BF16),
            pltpu.VMEM((2, CHUNKS, LANES, HEAD_DIM), BF16),
            pltpu.VMEM((2, CHUNKS, LANES, HEAD_DIM), BF16),
            pltpu.VMEM((2, CHUNKS, HEAD_DIM, LANES), BF16),
            pltpu.VMEM((2, CHUNKS, HEAD_DIM, LANES), BF16),
            pltpu.VMEM((slots, CHUNKS, BLOCK, LANES), F32),
            pltpu.VMEM((slots, CHUNKS, BLOCK, LANES), F32),
            pltpu.VMEM((CHUNKS, HEAD_DIM, LANES), F32),
            pltpu.VMEM((CHUNKS, HEAD_DIM, LANES), F32),
            pltpu.VMEM((2, CHUNKS, 1, LANES), F32),
            pltpu.VMEM((2, CHUNKS, 1, LANES), F32),
            pltpu.VMEM((2, CHUNKS, 1, LANES), F32),
            pltpu.VMEM((slots, CHUNKS, 1, LANES), F32),
            pltpu.VMEM((CHUNKS, 1, LANES), F32),
            pltpu.VMEM((2, CHUNKS, HEAD_DIM, LANES), F32),
            pltpu.VMEM((16, BLOCK, kv_width), F32),
        ],
        cost_estimate=pl.CostEstimate(
            flops=6 * 10**9, transcendentals=9 * 10**6, bytes_accessed=8 * 10**6
        ),
        compiler_params=pltpu.CompilerParams(vmem_limit_bytes=60 * 1024 * 1024),
    )(info, q_clean, g_clean, noisy, *pieces)


def columns_over_rows(mine, row_y):
    part = mine.shape[1] // 4
    received = []
    for k in range(4):
        pairs = [
            (2 * y + h, 2 * (2 * h + ((y ^ k) >> 1)) + ((y ^ k) & 1)) for y in range(4) for h in range(2)
        ]
        sent = lax.dynamic_slice_in_dim(mine, (row_y ^ k) * part, part, 1)
        received.append(lax.ppermute(sent, ("context_0", "head"), pairs))
    return received


def per_device(tokens, queries, grad_out, w_key, w_value, block_len):
    row_y = lax.axis_index("context_0")
    my_index = lax.axis_index(CONTEXT)
    head = lax.axis_index("head")
    shard_rows = tokens.shape[2]
    features = tokens.shape[3]
    width = queries.shape[3]
    rows = 2 * shard_rows
    over_rows = (((0,), (0,)), ((), ()))
    over_columns = (((1,), (1,)), ((), ()))
    weight_row = gather_z(jnp.concatenate([w_key, w_value], axis=1))
    received = columns_over_rows(tokens[0].reshape(rows, features), row_y)
    received[3], weight_row = lax.optimization_barrier((received[3], weight_row))
    here = jnp.concatenate(received, axis=0)
    there = jnp.concatenate([swapped(received[k ^ 1]) for k in range(4)], axis=0)
    base = 2 * (row_y & 1) + head
    half = weight_row.shape[0] // 2
    partial = dot(here, lax.dynamic_slice_in_dim(weight_row, head * half, half, 0)) + dot(
        there, lax.dynamic_slice_in_dim(weight_row, (1 - head) * half, half, 0)
    )

    def partial_for(step):
        return lax.dynamic_slice_in_dim(partial, (base ^ ((row_y + step) & 3)) * rows, rows, 0)

    whole = partial_for(0)
    for s in range(1, 4):
        whole = whole + shifted(partial_for(s).astype(BF16), "context_0", s).astype(F32)
    projected = whole.astype(BF16)

    noisy = jnp.concatenate([queries[0, 1], grad_out[0, 1], projected[shard_rows:]], axis=1)
    kv_row, noisy = lax.optimization_barrier(
        (gather_z(projected[:shard_rows]), turned_over(noisy, "context_0"))
    )
    kv_pieces = gather_ring(kv_row, "context_0")
    kv_pieces, noisy, weight_row = lax.optimization_barrier((kv_pieces, noisy, weight_row))
    weight_near = (shifted(weight_row, "context_0", 1), shifted(weight_row, "context_0", -1))

    block_size = block_len[0]
    shift = 3 + (block_size > 8).astype(jnp.int32) + (block_size > 16).astype(jnp.int32)
    rows_z = lax.axis_size("context_1")
    noisy_index = (3 - row_y) * rows_z + lax.axis_index("context_1")
    info = jnp.stack([row_y, my_index, noisy_index, shift]).astype(jnp.int32)
    dq_clean, returned, *pair_pieces = attention(
        info, queries[0, 0], grad_out[0, 0], noisy, kv_pieces
    )
    pair_pieces, returned, weight_near = lax.optimization_barrier(
        (pair_pieces, returned, weight_near)
    )
    pair_row, returned, weight_near = lax.optimization_barrier(
        (reduce_ring(pair_pieces, "context_0").astype(BF16), returned, weight_near)
    )
    before, after = weight_near
    weight_far = (shifted(before[:half], "context_0", 1), shifted(after[half:], "context_0", -1))
    pair_clean, returned, weight_far = lax.optimization_barrier(
        (scatter_z(pair_row).astype(BF16), turned_over(returned, "context_0"), weight_far)
    )
    dq_noisy, pair_noisy = returned[:, :width], returned[:, width:]
    pair_grads = jnp.concatenate([pair_clean, pair_noisy], axis=0)

    around = jnp.zeros((4 * rows, pair_grads.shape[1]), BF16)
    for s in range(4):
        piece = shifted(pair_grads, "context_0", s) if s else pair_grads
        around = lax.dynamic_update_slice_in_dim(
            around, piece, (base ^ ((row_y - s) & 3)) * rows, 0
        )
    local_here = lax.dot_general(here, around, over_rows, preferred_element_type=F32)
    local_there = lax.dot_general(there, around, over_rows, preferred_element_type=F32)
    weight_local = jnp.stack(
        [
            jnp.where(head == 0, local_here, local_there).astype(BF16),
            jnp.where(head == 0, local_there, local_here).astype(BF16),
        ]
    ).reshape(2 * half, -1)
    weight_local, pair_grads = lax.optimization_barrier((weight_local, pair_grads))
    other_pair, weight_row, before, after, weight_far = lax.optimization_barrier(
        (swapped(pair_grads), weight_row, before, after, weight_far)
    )
    weight_sum = scatter_z(weight_local).astype(BF16)
    copies = jnp.broadcast_to(weight_sum, (lax.axis_size("dp"), *weight_sum.shape))
    weight_sum = jnp.sum(lax.all_to_all(copies, "dp", 0, 0, tiled=True).astype(F32), axis=0)

    stacked = jnp.stack([weight_row, before, jnp.concatenate(weight_far, axis=0), after])

    def weight_half(which):
        return jnp.concatenate(
            [
                lax.dynamic_index_in_dim(stacked, (row_y - 2 * which - i) & 3, 0, keepdims=False)
                for i in range(2)
            ],
            axis=0,
        )

    kept = weight_half(head)
    given = swapped(weight_half(1 - head))
    grad_x = lax.dot_general(pair_grads, kept, over_columns, preferred_element_type=F32)
    grad_x = grad_x + lax.dot_general(
        other_pair, given, over_columns, preferred_element_type=F32
    )
    grad_x = grad_x.astype(BF16).reshape(tokens.shape)
    grad_query = jnp.stack([dq_clean, dq_noisy])[None]
    return (grad_query, grad_x, weight_sum[:, :HEAD_DIM], weight_sum[:, HEAD_DIM:])


def solution(mesh):
    torus = Mesh(
        mesh.devices.reshape(mesh.shape["dp"], 4, 8, mesh.shape["head"]),
        ("dp", "context_0", "context_1", "head"),
    )
    in_specs = (
        P("dp", None, CONTEXT, "head"),
        P("dp", None, CONTEXT, "head"),
        P("dp", None, CONTEXT, "head"),
        P(CONTEXT, "head"),
        P(CONTEXT, "head"),
        P("dp"),
    )
    out_specs = (
        P("dp", None, CONTEXT, "head"),
        P("dp", None, CONTEXT, "head"),
        P(CONTEXT, "head"),
        P(CONTEXT, "head"),
    )
    return jax.shard_map(
        per_device, mesh=torus, in_specs=in_specs, out_specs=out_specs, check_vma=False
    )
```

time: 228 us -> 223 us (0.978); the launches traced: 223 us -> 222 us
  starting transfers between devices: 65.4 us -> 88.1 us
  blocking collectives: 18.3 us -> 0 us
  waiting for transfers between devices: 87.4 us -> 81.6 us
  local copies, waits for them, and re-layouts: 7.57 us -> 11.7 us
  other arithmetic: 14.9 us -> 11.6 us
  Pallas kernels: 23.1 us -> 19.9 us
  matrix products: 4.95 us -> 7.59 us
    all_to_all x1 -> x0, blocking collectives: 18.3 us -> none  [gather_z(): tiles = lax.all_to_all(copies, 'context_1', 0, 0, tiled=True)]
    ppermute x16 -> x18, waiting for transfers between devices: 44.6 us -> 33.9 us  [shifted(): lax.ppermute(array, axis, [(i, (i + step) % size) for i in range(size)])]
    ppermute x1 -> x4, starting transfers between devices: 0.01 us -> 10.2 us  [columns_over_rows(): received.append(lax.ppermute(sent, ('context_0', 'head'), pairs))]
    all_to_all x1 -> x2, starting transfers between devices: 9.15 us -> 16.1 us  [gather_z(): tiles = lax.all_to_all(copies, 'context_1', 0, 0, tiled=True)]
    ppermute x1 -> x4, waiting for transfers between devices: 0.01 us -> 6.06 us  [columns_over_rows(): received.append(lax.ppermute(sent, ('context_0', 'head'), pairs))]
    all_to_all x2, starting transfers between devices: 9.82 us -> 15.9 us  [scatter_z(): tiles = lax.all_to_all(tiles, 'context_1', 0, 0, tiled=True)]
    all_to_all x2, waiting for transfers between devices: 23 us -> 19.3 us  [scatter_z(): tiles = lax.all_to_all(tiles, 'context_1', 0, 0, tiled=True)]
    convert_element_type x5 -> x3, other arithmetic: 6.97 us -> 3.25 us  [the longest x1 1.11 us: reduce_ring(): from_after = shifted(down.astype(BF16), axis, -1)]
  transfers between devices with their start and end apart: 27 -> 35, of which waited for: 15 -> 19; matrix products, arithmetic and copies ran while one was open for 9% -> 6% of each run, Pallas kernels for 0% -> 9%
where the time goes in v2:
time: 223 us; the launch traced here: 222 us
  starting transfers between devices  88.1 us (40%)
  waiting for transfers between devices  81.6 us (37%)
  Pallas kernels  19.9 us (9%)
  local copies, waits for them, and re-layouts  11.7 us (5%)
  other arithmetic  11.6 us (5%)
  matrix products  7.59 us (3%)
    ppermute x18, waiting for transfers between devices, shifted(): lax.ppermute(array, axis, [(i, (i + step) % size) for i in range(size)])  33.9 us
    ppermute x18, starting transfers between devices, shifted(): lax.ppermute(array, axis, [(i, (i + step) % size) for i in range(size)])  22.9 us
    pallas_call x1, Pallas kernels, attention(): pl.pallas_call(attention_kernel, out_shape=(shape((rows, width), BF16), s...  19.9 us
    all_to_all x2, waiting for transfers between devices, scatter_z(): tiles = lax.all_to_all(tiles, 'context_1', 0, 0, tiled=True)  19.3 us
    all_to_all x2, starting transfers between devices, gather_z(): tiles = lax.all_to_all(copies, 'context_1', 0, 0, tiled=True)  16.1 us
    ppermute x6, starting transfers between devices, swapped(): return lax.ppermute(array, 'head', [(0, 1), (1, 0)])  16 us
    all_to_all x2, starting transfers between devices, scatter_z(): tiles = lax.all_to_all(tiles, 'context_1', 0, 0, tiled=True)  15.9 us
    ppermute x2, waiting for transfers between devices, turned_over(): return lax.ppermute(array, axis, [(i, size - 1 - i) for i in range(size)])  14.6 us
  transfers between devices with their start and end apart: 35, of which 19 were waited for; matrix products, arithmetic and copies ran while one was open for 6% of the time, Pallas kernels for 9%

profile of v2, /device:TPU:1, one launch (start us, length us, event | category | flops | bytes accessed | tf_op | source)
XLA Modules:
  0.0 222.2 jit_solution(7397632261686037172)
XLA Ops:
  2.3 9.0 %all-to-all-start = ((bf16[8,128,256]{2,1,0:T(8,128)(2,1)}), bf16[8,128,256]{2,1,0:T(8,128)(2,1)S(1)}, u32[]{:S(2)}, u32[]{:S(2)}) async-start(bf16[8,128,256]{2,1,0:T(8,128)(2,1)} %broadcast_in_dim.15), calls=%async_computation | async-start | bytes 1048576 | tf_op jit(solution)/shard_map/all_to_all | solution.py:44
  11.5 3.0 %collective-permute-start.1 = (bf16[256,512]{1,0:T(8,128)(2,1)S(1)}, bf16[256,512]{1,0:T(8,128)(2,1)S(1)}, u32[]{:S(2)}, u32[]{:S(2)}) collective-permute-start(bf16[256,512]{1,0:T(8,128)(2,1)S(1)} %get-tuple-element.97), channel_id=1, source_target_pairs={{0,1},{1,33},{16,0},{17,32},{32,17},{33,49},{48,16},{49,48},{2,3},... | collective-permute-start | bytes 786440 | tf_op jit(solution)/shard_map/ppermute | solution.py:325
  14.5 2.8 %collective-permute-start = (bf16[256,512]{1,0:T(8,128)(2,1)S(1)}, bf16[256,512]{1,0:T(8,128)(2,1)S(1)}, u32[]{:S(2)}, u32[]{:S(2)}) collective-permute-start(bf16[256,512]{1,0:T(8,128)(2,1)S(1)} %get-tuple-element.98), channel_id=1, source_target_pairs={{0,0},{1,32},{16,1},{17,33},{32,16},{33,48},{48,17},{49,49},{2,2},... | collective-permute-start | bytes 786440 | tf_op jit(solution)/shard_map/ppermute | solution.py:325
  42.0 4.9 %collective-permute-done.8 = bf16[256,256]{1,0:T(8,128)(2,1)} collective-permute-done((bf16[256,256]{1,0:T(8,128)(2,1)S(1)}, bf16[256,256]{1,0:T(8,128)(2,1)}, u32[]{:S(2)}, u32[]{:S(2)}) %collective-permute-start.8) | collective-permute-done | bytes 131104 | tf_op jit(solution)/shard_map/ppermute | solution.py:30
  48.7 7.1 %all-to-all-start.1 = ((bf16[8,128,256]{2,1,0:T(8,128)(2,1)}), bf16[8,128,256]{2,1,0:T(8,128)(2,1)}, u32[]{:S(2)}, u32[]{:S(2)}) async-start(bf16[8,128,256]{2,1,0:T(8,128)(2,1)} %broadcast_in_dim.16), calls=%async_computation.1 | async-start | bytes 1048576 | tf_op jit(solution)/shard_map/all_to_all | solution.py:44
  55.9 14.6 %collective-permute-done.11.noisy = bf16[128,2304]{1,0:T(8,128)(2,1)} collective-permute-done((bf16[128,2304]{1,0:T(8,128)(2,1)S(1)}, bf16[128,2304]{1,0:T(8,128)(2,1)}, u32[]{:S(2)}, u32[]{:S(2)}) %collective-permute-start.11) | collective-permute-done | bytes 589856 | tf_op jit(solution)/shard_map/ppermute | solution.py:35
  72.3 2.7 %collective-permute-start.14 = (bf16[1024,256]{1,0:T(8,128)(2,1)}, bf16[1024,256]{1,0:T(8,128)(2,1)S(1)}, u32[]{:S(2)}, u32[]{:S(2)}) collective-permute-start(bf16[1024,256]{1,0:T(8,128)(2,1)} %bitcast.7.kv_0), channel_id=1, source_target_pairs={{0,48},{16,0},{32,16},{48,32},{1,49},{17,1},{33,17},{49,33},{2,50}... | collective-permute-start | bytes 1572872 | tf_op jit(solution)/shard_map/ppermute | solution.py:30
  75.0 10.1 %collective-permute-done.12.kv_1 = bf16[1024,256]{1,0:T(8,128)(2,1)S(1)} collective-permute-done((bf16[1024,256]{1,0:T(8,128)(2,1)}, bf16[1024,256]{1,0:T(8,128)(2,1)S(1)}, u32[]{:S(2)}, u32[]{:S(2)}) %collective-permute-start.12) | collective-permute-done | bytes 524320 | tf_op jit(solution)/shard_map/ppermute | solution.py:30
  92.2 3.2 %collective-permute-start.17 = (bf16[1024,256]{1,0:T(8,128)(2,1)S(1)}, bf16[1024,256]{1,0:T(8,128)(2,1)S(1)}, u32[]{:S(2)}, u32[]{:S(2)}) collective-permute-start(bf16[1024,256]{1,0:T(8,128)(2,1)S(1)} %bitcast.52), channel_id=1, source_target_pairs={{0,48},{16,0},{32,16},{48,32},{1,49},{17,1},{33,17},{49,33},{2,50}... | collective-permute-start | bytes 1572872 | tf_op jit(solution)/shard_map/ppermute | solution.py:30
  95.4 19.9 %shard_map.93 = (bf16[128,1024]{1,0:T(8,128)(2,1)}, bf16[128,1280]{1,0:T(8,128)(2,1)}, bf16[1024,256]{1,0:T(8,128)(2,1)}, bf16[1024,256]{1,0:T(8,128)(2,1)}, bf1...) custom-call(s32[4]{0:T(128)} %pad_add_fusion.info, ...), custom_call_target="tpu_custom_call" | custom-call | flops 6000000000 | bytes 8000000 | tf_op jit(solution)/shard_map/pallas_call | solution.py:279
  118.1 4.0 %collective-permute-done.18 = bf16[512,256]{1,0:T(8,128)(2,1)S(1)} collective-permute-done((bf16[512,256]{1,0:T(8,128)(2,1)}, bf16[512,256]{1,0:T(8,128)(2,1)S(1)}, u32[]{:S(2)}, u32[]{:S(2)}) %collective-permute-start.18) | collective-permute-done | bytes 262176 | tf_op jit(solution)/shard_map/ppermute | solution.py:30
  124.4 2.7 %collective-permute-start.21 = (bf16[1024,256]{1,0:T(8,128)(2,1)S(1)}, bf16[1024,256]{1,0:T(8,128)(2,1)S(1)}, u32[]{:S(2)}, u32[]{:S(2)}) collective-permute-start(bf16[1024,256]{1,0:T(8,128)(2,1)S(1)} %add_convert_fusion.1), channel_id=1, source_target_pairs={{0,48},{16,0},{32,16},{48,32},{1,49},{17,1},{33,17},{49,33},{2,50}... | collective-permute-start | bytes 1572872 | tf_op jit(solution)/shard_map/ppermute | solution.py:30
  127.1 6.0 %collective-permute-done.19 = bf16[1024,256]{1,0:T(8,128)(2,1)S(1)} collective-permute-done((bf16[1024,256]{1,0:T(8,128)(2,1)S(1)}, bf16[1024,256]{1,0:T(8,128)(2,1)S(1)}, u32[]{:S(2)}, u32[]{:S(2)}) %collective-permute-start.19) | collective-permute-done | bytes 524320 | tf_op jit(solution)/shard_map/ppermute | solution.py:30
  134.3 10.0 %all-to-all-start.2 = ((bf16[8,128,256]{2,1,0:T(8,128)(2,1)}), bf16[8,128,256]{2,1,0:T(8,128)(2,1)S(1)}, u32[]{:S(2)}, u32[]{:S(2)}) async-start(bf16[8,128,256]{2,1,0:T(8,128)(2,1)} %bitcast.11), calls=%async_computation.2 | async-start | bytes 1048576 | tf_op jit(solution)/shard_map/all_to_all | solution.py:72
  144.3 3.0 %collective-permute-start.22 = (bf16[128,1280]{1,0:T(8,128)(2,1)}, bf16[128,1280]{1,0:T(8,128)(2,1)S(1)}, u32[]{:S(2)}, u32[]{:S(2)}) collective-permute-start(bf16[128,1280]{1,0:T(8,128)(2,1)} %get-tuple-element.73), channel_id=1, source_target_pairs={{0,48},{16,32},{32,16},{48,0},{1,49},{17,33},{33,17},{49,1},{2,50}... | collective-permute-start | bytes 983048 | tf_op jit(solution)/shard_map/ppermute | solution.py:35
  151.4 5.0 %all-to-all-done.2 = bf16[8,128,256]{2,1,0:T(8,128)(2,1)S(1)} async-done(((bf16[8,128,256]{2,1,0:T(8,128)(2,1)}), bf16[8,128,256]{2,1,0:T(8,128)(2,1)S(1)}, u32[]{:S(2)}, u32[]{:S(2)}) %all-to-all-start.2) | async-done | bytes 524320 | tf_op jit(solution)/shard_map/all_to_all | solution.py:72
  159.1 4.1 %collective-permute-start.26 = (bf16[256,256]{1,0:T(8,128)(2,1)S(1)}, bf16[256,256]{1,0:T(8,128)(2,1)S(1)}, u32[]{:S(2)}, u32[]{:S(2)}) collective-permute-start(bf16[256,256]{1,0:T(8,128)(2,1)S(1)} %get-tuple-element.78), channel_id=1, source_target_pairs={{0,32},{16,48},{32,0},{48,16},{1,33},{17,49},{33,1},{49,17},{2,34}... | collective-permute-start | bytes 393224 | tf_op jit(solution)/shard_map/ppermute | solution.py:30
  163.2 4.4 %collective-permute-done.25 = bf16[256,256]{1,0:T(8,128)(2,1)S(1)} collective-permute-done((bf16[256,256]{1,0:T(8,128)(2,1)S(1)}, bf16[256,256]{1,0:T(8,128)(2,1)S(1)}, u32[]{:S(2)}, u32[]{:S(2)}) %collective-permute-start.25) | collective-permute-done | bytes 131104 | tf_op jit(solution)/shard_map/ppermute | solution.py:30
  171.3 13.1 %collective-permute-start.28 = (bf16[256,256]{1,0:T(8,128)(2,1)S(1)}, bf16[256,256]{1,0:T(8,128)(2,1)S(1)}, u32[]{:S(2)}, u32[]{:S(2)}) collective-permute-start(bf16[256,256]{1,0:T(8,128)(2,1)S(1)} %get-tuple-element.78), channel_id=1, source_target_pairs={{0,1},{1,0},{2,3},{3,2},{4,5},{5,4},{6,7},{7,6},{8,9},{9,8},{10,11... | collective-permute-start | bytes 393224 | tf_op jit(solution)/shard_map/ppermute | solution.py:39
  184.4 5.8 %all-to-all-start.3 = ((bf16[8,128,256]{2,1,0:T(8,128)(2,1)}), bf16[8,128,256]{2,1,0:T(8,128)(2,1)S(1)}, u32[]{:S(2)}, u32[]{:S(2)}) async-start(bf16[8,128,256]{2,1,0:T(8,128)(2,1)} %bitcast.26), calls=%async_computation.3 | async-start | bytes 1048576 | tf_op jit(solution)/shard_map/all_to_all | solution.py:72
  194.0 14.2 %all-to-all-done.3 = bf16[8,128,256]{2,1,0:T(8,128)(2,1)S(1)} async-done(((bf16[8,128,256]{2,1,0:T(8,128)(2,1)}), bf16[8,128,256]{2,1,0:T(8,128)(2,1)S(1)}, u32[]{:S(2)}, u32[]{:S(2)}) %all-to-all-start.3) | async-done | bytes 524320 | tf_op jit(solution)/shard_map/all_to_all | solution.py:72
  209.0 4.0 %all-to-all-start.4 = ((bf16[4,128,256]{2,1,0:T(8,128)(2,1)}), bf16[4,128,256]{2,1,0:T(8,128)(2,1)S(1)}, u32[]{:S(2)}, u32[]{:S(2)}) async-start(bf16[4,128,256]{2,1,0:T(8,128)(2,1)} %broadcast_in_dim.19), calls=%async_computation.4 | async-start | bytes 524288 | tf_op jit(solution)/shard_map/all_to_all | solution.py:408
  213.5 5.2 %all-to-all-done.4 = bf16[4,128,256]{2,1,0:T(8,128)(2,1)S(1)} async-done(((bf16[4,128,256]{2,1,0:T(8,128)(2,1)}), bf16[4,128,256]{2,1,0:T(8,128)(2,1)S(1)}, u32[]{:S(2)}, u32[]{:S(2)}) %all-to-all-start.4) | async-done | bytes 262176 | tf_op jit(solution)/shard_map/all_to_all | solution.py:408
  219.5 2.7 %fusion = bf16[256,2048]{1,0:T(8,128)(2,1)} fusion(f32[256,2048]{1,0:T(8,128)S(1)} %fusion.1, bf16[256,256]{1,0:T(8,128)(2,1)} %copy-done.7, bf16[2048,256]{1,0:T(8,128)(2,1)} %collective-permute-done.29), kind=kOutput, calls=%fused_computation.1 | convolution fusion | flops 269484032 | bytes 4325376 | tf_op jit(solution)/shard_map/dot_general | solution.py:424
  (118 shorter events, 58.8 us)
Async XLA Ops:
  2.3 27.1 %all-to-all-start = ((bf16[8,128,256]{2,1,0:T(8,128)(2,1)}), bf16[8,128,256]{2,1,0:T(8,128)(2,1)S(1)}, u32[]{:S(2)}, u32[]{:S(2)}) async-start(bf16[8,128,256]{2,1,0:T(8,128)(2,1)} %broadcast_in_dim.15), calls=%async_computation | async-start | bytes 1048576 | tf_op jit(solution)/shard_map/all_to_all | solution.py:44
  11.5 10.3 %collective-permute-start.1 = (bf16[256,512]{1,0:T(8,128)(2,1)S(1)}, bf16[256,512]{1,0:T(8,128)(2,1)S(1)}, u32[]{:S(2)}, u32[]{:S(2)}) collective-permute-start(bf16[256,512]{1,0:T(8,128)(2,1)S(1)} %get-tuple-element.97), channel_id=1, source_target_pairs={{0,1},{1,33},{16,0},{17,32},{32,17},{33,49},{48,16},{49,48},{2,3},... | collective-permute-start | bytes 786440 | tf_op jit(solution)/shard_map/ppermute | solution.py:325
  14.5 9.7 %collective-permute-start = (bf16[256,512]{1,0:T(8,128)(2,1)S(1)}, bf16[256,512]{1,0:T(8,128)(2,1)S(1)}, u32[]{:S(2)}, u32[]{:S(2)}) collective-permute-start(bf16[256,512]{1,0:T(8,128)(2,1)S(1)} %get-tuple-element.98), channel_id=1, source_target_pairs={{0,0},{1,32},{16,1},{17,33},{32,16},{33,48},{48,17},{49,49},{2,2},... | collective-permute-start | bytes 786440 | tf_op jit(solution)/shard_map/ppermute | solution.py:325
  17.2 9.4 %collective-permute-start.2 = (bf16[256,512]{1,0:T(8,128)(2,1)S(1)}, bf16[256,512]{1,0:T(8,128)(2,1)S(1)}, u32[]{:S(2)}, u32[]{:S(2)}) collective-permute-start(bf16[256,512]{1,0:T(8,128)(2,1)S(1)} %get-tuple-element.96), channel_id=1, source_target_pairs={{0,16},{1,48},{16,17},{17,49},{32,0},{33,32},{48,1},{49,33},{2,18}... | collective-permute-start | bytes 786440 | tf_op jit(solution)/shard_map/ppermute | solution.py:325
  19.7 9.8 %collective-permute-start.3 = (bf16[256,512]{1,0:T(8,128)(2,1)S(1)}, bf16[256,512]{1,0:T(8,128)(2,1)S(1)}, u32[]{:S(2)}, u32[]{:S(2)}) collective-permute-start(bf16[256,512]{1,0:T(8,128)(2,1)S(1)} %get-tuple-element.95), channel_id=1, source_target_pairs={{0,17},{1,49},{16,16},{17,48},{32,1},{33,33},{48,0},{49,32},{2,19}... | collective-permute-start | bytes 786440 | tf_op jit(solution)/shard_map/ppermute | solution.py:325
  38.0 8.8 %collective-permute-start.8 = (bf16[256,256]{1,0:T(8,128)(2,1)S(1)}, bf16[256,256]{1,0:T(8,128)(2,1)}, u32[]{:S(2)}, u32[]{:S(2)}) collective-permute-start(bf16[256,256]{1,0:T(8,128)(2,1)S(1)} %get-tuple-element.92), channel_id=1, source_target_pairs={{0,16},{16,32},{32,48},{48,0},{1,17},{17,33},{33,49},{49,1},{2,18}... | collective-permute-start | bytes 393224 | tf_op jit(solution)/shard_map/ppermute | solution.py:30
  48.7 23.6 %all-to-all-start.1 = ((bf16[8,128,256]{2,1,0:T(8,128)(2,1)}), bf16[8,128,256]{2,1,0:T(8,128)(2,1)}, u32[]{:S(2)}, u32[]{:S(2)}) async-start(bf16[8,128,256]{2,1,0:T(8,128)(2,1)} %broadcast_in_dim.16), calls=%async_computation.1 | async-start | bytes 1048576 | tf_op jit(solution)/shard_map/all_to_all | solution.py:44
  55.8 14.7 %collective-permute-start.11 = (bf16[128,2304]{1,0:T(8,128)(2,1)S(1)}, bf16[128,2304]{1,0:T(8,128)(2,1)}, u32[]{:S(2)}, u32[]{:S(2)}) collective-permute-start(bf16[128,2304]{1,0:T(8,128)(2,1)S(1)} %pad_maximum_fusion.2), channel_id=1, source_target_pairs={{0,48},{16,32},{32,16},{48,0},{1,49},{17,33},{33,17},{49,1},{2,50}... | collective-permute-start | bytes 1769480 | tf_op jit(solution)/shard_map/ppermute | solution.py:35
  72.3 12.8 %collective-permute-start.12 = (bf16[1024,256]{1,0:T(8,128)(2,1)}, bf16[1024,256]{1,0:T(8,128)(2,1)S(1)}, u32[]{:S(2)}, u32[]{:S(2)}) collective-permute-start(bf16[1024,256]{1,0:T(8,128)(2,1)} %bitcast.7.kv_0), channel_id=1, source_target_pairs={{0,16},{16,32},{32,48},{48,0},{1,17},{17,33},{33,49},{49,1},{2,18}... | collective-permute-start | bytes 1572872 | tf_op jit(solution)/shard_map/ppermute | solution.py:30
  72.3 13.6 %collective-permute-start.14 = (bf16[1024,256]{1,0:T(8,128)(2,1)}, bf16[1024,256]{1,0:T(8,128)(2,1)S(1)}, u32[]{:S(2)}, u32[]{:S(2)}) collective-permute-start(bf16[1024,256]{1,0:T(8,128)(2,1)} %bitcast.7.kv_0), channel_id=1, source_target_pairs={{0,48},{16,0},{32,16},{48,32},{1,49},{17,1},{33,17},{49,33},{2,50}... | collective-permute-start | bytes 1572872 | tf_op jit(solution)/shard_map/ppermute | solution.py:30
  92.2 23.2 %collective-permute-start.16 = (bf16[1024,256]{1,0:T(8,128)(2,1)S(1)}, bf16[1024,256]{1,0:T(8,128)(2,1)S(1)}, u32[]{:S(2)}, u32[]{:S(2)}) collective-permute-start(bf16[1024,256]{1,0:T(8,128)(2,1)S(1)} %bitcast.51), channel_id=1, source_target_pairs={{0,16},{16,32},{32,48},{48,0},{1,17},{17,33},{33,49},{49,1},{2,18}... | collective-permute-start | bytes 1572872 | tf_op jit(solution)/shard_map/ppermute | solution.py:30
  92.2 23.2 %collective-permute-start.17 = (bf16[1024,256]{1,0:T(8,128)(2,1)S(1)}, bf16[1024,256]{1,0:T(8,128)(2,1)S(1)}, u32[]{:S(2)}, u32[]{:S(2)}) collective-permute-start(bf16[1024,256]{1,0:T(8,128)(2,1)S(1)} %bitcast.52), channel_id=1, source_target_pairs={{0,48},{16,0},{32,16},{48,32},{1,49},{17,1},{33,17},{49,33},{2,50}... | collective-permute-start | bytes 1572872 | tf_op jit(solution)/shard_map/ppermute | solution.py:30
  123.2 9.9 %collective-permute-start.19 = (bf16[1024,256]{1,0:T(8,128)(2,1)S(1)}, bf16[1024,256]{1,0:T(8,128)(2,1)S(1)}, u32[]{:S(2)}, u32[]{:S(2)}) collective-permute-start(bf16[1024,256]{1,0:T(8,128)(2,1)S(1)} %add_convert_fusion.2), channel_id=1, source_target_pairs={{0,16},{16,32},{32,48},{48,0},{1,17},{17,33},{33,49},{49,1},{2,18}... | collective-permute-start | bytes 1572872 | tf_op jit(solution)/shard_map/ppermute | solution.py:30
  124.4 8.9 %collective-permute-start.21 = (bf16[1024,256]{1,0:T(8,128)(2,1)S(1)}, bf16[1024,256]{1,0:T(8,128)(2,1)S(1)}, u32[]{:S(2)}, u32[]{:S(2)}) collective-permute-start(bf16[1024,256]{1,0:T(8,128)(2,1)S(1)} %add_convert_fusion.1), channel_id=1, source_target_pairs={{0,48},{16,0},{32,16},{48,32},{1,49},{17,1},{33,17},{49,33},{2,50}... | collective-permute-start | bytes 1572872 | tf_op jit(solution)/shard_map/ppermute | solution.py:30
  134.3 22.2 %all-to-all-start.2 = ((bf16[8,128,256]{2,1,0:T(8,128)(2,1)}), bf16[8,128,256]{2,1,0:T(8,128)(2,1)S(1)}, u32[]{:S(2)}, u32[]{:S(2)}) async-start(bf16[8,128,256]{2,1,0:T(8,128)(2,1)} %bitcast.11), calls=%async_computation.2 | async-start | bytes 1048576 | tf_op jit(solution)/shard_map/all_to_all | solution.py:72
  144.3 12.9 %collective-permute-start.22 = (bf16[128,1280]{1,0:T(8,128)(2,1)}, bf16[128,1280]{1,0:T(8,128)(2,1)S(1)}, u32[]{:S(2)}, u32[]{:S(2)}) collective-permute-start(bf16[128,1280]{1,0:T(8,128)(2,1)} %get-tuple-element.73), channel_id=1, source_target_pairs={{0,48},{16,32},{32,16},{48,0},{1,49},{17,33},{33,17},{49,1},{2,50}... | collective-permute-start | bytes 983048 | tf_op jit(solution)/shard_map/ppermute | solution.py:35
  148.0 9.2 %collective-permute-start.23 = (bf16[512,256]{1,0:T(8,128)(2,1)}, bf16[512,256]{1,0:T(8,128)(2,1)}, u32[]{:S(2)}, u32[]{:S(2)}) collective-permute-start(bf16[512,256]{1,0:T(8,128)(2,1)} %slice.50), channel_id=1, source_target_pairs={{0,16},{16,32},{32,48},{48,0},{1,17},{17,33},{33,49},{49,1},{2,18}... | collective-permute-start | bytes 786440 | tf_op jit(solution)/shard_map/ppermute | solution.py:30
  148.7 8.4 %collective-permute-start.24 = (bf16[512,256]{1,0:T(8,128)(2,1)}, bf16[512,256]{1,0:T(8,128)(2,1)}, u32[]{:S(2)}, u32[]{:S(2)}) collective-permute-start(bf16[512,256]{1,0:T(8,128)(2,1)} %slice.51), channel_id=1, source_target_pairs={{0,48},{16,0},{32,16},{48,32},{1,49},{17,1},{33,17},{49,33},{2,50}... | collective-permute-start | bytes 786440 | tf_op jit(solution)/shard_map/ppermute | solution.py:30
  158.8 8.8 %collective-permute-start.25 = (bf16[256,256]{1,0:T(8,128)(2,1)S(1)}, bf16[256,256]{1,0:T(8,128)(2,1)S(1)}, u32[]{:S(2)}, u32[]{:S(2)}) collective-permute-start(bf16[256,256]{1,0:T(8,128)(2,1)S(1)} %get-tuple-element.78), channel_id=1, source_target_pairs={{0,16},{16,32},{32,48},{48,0},{1,17},{17,33},{33,49},{49,1},{2,18}... | collective-permute-start | bytes 393224 | tf_op jit(solution)/shard_map/ppermute | solution.py:30
  159.1 8.5 %collective-permute-start.26 = (bf16[256,256]{1,0:T(8,128)(2,1)S(1)}, bf16[256,256]{1,0:T(8,128)(2,1)S(1)}, u32[]{:S(2)}, u32[]{:S(2)}) collective-permute-start(bf16[256,256]{1,0:T(8,128)(2,1)S(1)} %get-tuple-element.78), channel_id=1, source_target_pairs={{0,32},{16,48},{32,0},{48,16},{1,33},{17,49},{33,1},{49,17},{2,34}... | collective-permute-start | bytes 393224 | tf_op jit(solution)/shard_map/ppermute | solution.py:30
  171.3 18.9 %collective-permute-start.28 = (bf16[256,256]{1,0:T(8,128)(2,1)S(1)}, bf16[256,256]{1,0:T(8,128)(2,1)S(1)}, u32[]{:S(2)}, u32[]{:S(2)}) collective-permute-start(bf16[256,256]{1,0:T(8,128)(2,1)S(1)} %get-tuple-element.78), channel_id=1, source_target_pairs={{0,1},{1,0},{2,3},{3,2},{4,5},{5,4},{6,7},{7,6},{8,9},{9,8},{10,11... | collective-permute-start | bytes 393224 | tf_op jit(solution)/shard_map/ppermute | solution.py:39
  184.4 23.9 %all-to-all-start.3 = ((bf16[8,128,256]{2,1,0:T(8,128)(2,1)}), bf16[8,128,256]{2,1,0:T(8,128)(2,1)S(1)}, u32[]{:S(2)}, u32[]{:S(2)}) async-start(bf16[8,128,256]{2,1,0:T(8,128)(2,1)} %bitcast.26), calls=%async_computation.3 | async-start | bytes 1048576 | tf_op jit(solution)/shard_map/all_to_all | solution.py:72
  192.8 26.6 %collective-permute-start.29 = (bf16[2048,256]{1,0:T(8,128)(2,1)}, bf16[2048,256]{1,0:T(8,128)(2,1)}, u32[]{:S(2)}, u32[]{:S(2)}) collective-permute-start(bf16[2048,256]{1,0:T(8,128)(2,1)} %pad_maximum_fusion.1), channel_id=1, source_target_pairs={{0,1},{1,0},{2,3},{3,2},{4,5},{5,4},{6,7},{7,6},{8,9},{9,8},{10,11... | collective-permute-start | bytes 3145736 | tf_op jit(solution)/shard_map/ppermute | solution.py:39
  209.0 9.7 %all-to-all-start.4 = ((bf16[4,128,256]{2,1,0:T(8,128)(2,1)}), bf16[4,128,256]{2,1,0:T(8,128)(2,1)S(1)}, u32[]{:S(2)}, u32[]{:S(2)}) async-start(bf16[4,128,256]{2,1,0:T(8,128)(2,1)} %broadcast_in_dim.19), calls=%async_computation.4 | async-start | bytes 524288 | tf_op jit(solution)/shard_map/all_to_all | solution.py:408
  (22 other events, 112.0 us)

commit v3 on v2

--- a/solution.py
+++ b/solution.py
@@ -314,6 +314,33 @@
     )(info, q_clean, g_clean, noisy, *pieces)
 
 
+def halves_kernel(info, own, before, far_low, far_high, after, kept, given):
+    row_y = info[0]
+    head = info[1]
+    span = own.shape[0]
+    half = span // 2
+    for part, sources in enumerate(((own,), (before,), (far_low, far_high), (after,))):
+        block = (row_y - part) & 3
+        place = block & 1
+        for target, wanted in ((kept, head), (given, 1 - head)):
+
+            @pl.when((block >> 1) == wanted)
+            def _():
+                for i, source in enumerate(sources):
+                    target[place, i * half : i * half + source.shape[0], :] = source[...]
+
+
+def weight_halves(row_y, head, own, before, far_low, far_high, after):
+    vmem = pl.BlockSpec(memory_space=pltpu.VMEM)
+    shape = jax.ShapeDtypeStruct((2, *own.shape), BF16)
+    return pl.pallas_call(
+        halves_kernel,
+        out_shape=(shape, shape),
+        in_specs=[pl.BlockSpec(memory_space=pltpu.SMEM)] + [vmem] * 5,
+        out_specs=(vmem, vmem),
+    )(jnp.stack([row_y, head]).astype(jnp.int32), own, before, far_low, far_high, after)
+
+
 def columns_over_rows(mine, row_y):
     part = mine.shape[1] // 4
     received = []
@@ -334,6 +361,7 @@
     features = tokens.shape[3]
     width = queries.shape[3]
     rows = 2 * shard_rows
+    kv_width = 2 * HEAD_DIM
     over_rows = (((0,), (0,)), ((), ()))
     over_columns = (((1,), (1,)), ((), ()))
     weight_row = gather_z(jnp.concatenate([w_key, w_value], axis=1))
@@ -391,6 +419,8 @@
         around = lax.dynamic_update_slice_in_dim(
             around, piece, (base ^ ((row_y - s) & 3)) * rows, 0
         )
+    kept, given = weight_halves(row_y, head, weight_row, before, *weight_far, after)
+    around, kept, given = lax.optimization_barrier((around, kept, given))
     local_here = lax.dot_general(here, around, over_rows, preferred_element_type=F32)
     local_there = lax.dot_general(there, around, over_rows, preferred_element_type=F32)
     weight_local = jnp.stack(
@@ -400,33 +430,23 @@
         ]
     ).reshape(2 * half, -1)
     weight_local, pair_grads = lax.optimization_barrier((weight_local, pair_grads))
-    other_pair, weight_row, before, after, weight_far = lax.optimization_barrier(
-        (swapped(pair_grads), weight_row, before, after, weight_far)
-    )
-    weight_sum = scatter_z(weight_local).astype(BF16)
+    other_pair = swapped(pair_grads)
+    given = swapped(given)
+    weight_sum, given = lax.optimization_barrier((scatter_z(weight_local).astype(BF16), given))
+    kept = kept.reshape(features, kv_width)
+    given = given.reshape(features, kv_width)
     copies = jnp.broadcast_to(weight_sum, (lax.axis_size("dp"), *weight_sum.shape))
-    weight_sum = jnp.sum(lax.all_to_all(copies, "dp", 0, 0, tiled=True).astype(F32), axis=0)
-
-    stacked = jnp.stack([weight_row, before, jnp.concatenate(weight_far, axis=0), after])
-
-    def weight_half(which):
-        return jnp.concatenate(
-            [
-                lax.dynamic_index_in_dim(stacked, (row_y - 2 * which - i) & 3, 0, keepdims=False)
-                for i in range(2)
-            ],
-            axis=0,
-        )
-
-    kept = weight_half(head)
-    given = swapped(weight_half(1 - head))
+    weight_tiles = lax.all_to_all(copies, "dp", 0, 0, tiled=True)
+    weight_sums = [
+        jnp.sum(weight_tiles[..., at : at + HEAD_DIM].astype(F32), axis=0) for at in (0, HEAD_DIM)
+    ]
     grad_x = lax.dot_general(pair_grads, kept, over_columns, preferred_element_type=F32)
     grad_x = grad_x + lax.dot_general(
         other_pair, given, over_columns, preferred_element_type=F32
     )
     grad_x = grad_x.astype(BF16).reshape(tokens.shape)
     grad_query = jnp.stack([dq_clean, dq_noisy])[None]
-    return (grad_query, grad_x, weight_sum[:, :HEAD_DIM], weight_sum[:, HEAD_DIM:])
+    return (grad_query, grad_x, *weight_sums)
 
 
 def solution(mesh):

time: 223 us -> 218 us (0.978)
  waiting for transfers between devices: 81.6 us -> 77.3 us
  Pallas kernels: 19.9 us -> 23 us
  local copies, waits for them, and re-layouts: 11.7 us -> 8.95 us
  other arithmetic: 11.6 us -> 8.92 us
    pallas_call x0 -> x1, Pallas kernels: none -> 3.06 us  [weight_halves(): pl.pallas_call(halves_kernel, out_shape=(shape, shape), in_specs=[pl.Bloc...]
    ppermute x18, waiting for transfers between devices: 33.9 us -> 31.3 us  [shifted(): lax.ppermute(array, axis, [(i, (i + step) % size) for i in range(size)])]
  transfers between devices with their start and end apart: 35 -> 35, of which waited for: 19 -> 18; matrix products, arithmetic and copies ran while one was open for 6% -> 8% of each run, Pallas kernels for 9% -> 11%
where the time goes in v3:
time: 218 us; the launch traced here: 217 us
  starting transfers between devices  88.3 us (41%)
  waiting for transfers between devices  77.3 us (35%)
  Pallas kernels  23 us (11%)
  local copies, waits for them, and re-layouts  8.95 us (4%)
  other arithmetic  8.92 us (4%)
  matrix products  8.74 us (4%)
    ppermute x18, waiting for transfers between devices, shifted(): lax.ppermute(array, axis, [(i, (i + step) % size) for i in range(size)])  31.3 us
    ppermute x18, starting transfers between devices, shifted(): lax.ppermute(array, axis, [(i, (i + step) % size) for i in range(size)])  24 us
    all_to_all x2, waiting for transfers between devices, scatter_z(): tiles = lax.all_to_all(tiles, 'context_1', 0, 0, tiled=True)  20.8 us
    pallas_call x1, Pallas kernels, attention(): pl.pallas_call(attention_kernel, out_shape=(shape((rows, width), BF16), s...  20 us
    all_to_all x2, starting transfers between devices, scatter_z(): tiles = lax.all_to_all(tiles, 'context_1', 0, 0, tiled=True)  16.4 us
    all_to_all x2, starting transfers between devices, gather_z(): tiles = lax.all_to_all(copies, 'context_1', 0, 0, tiled=True)  16 us
    ppermute x2, waiting for transfers between devices, turned_over(): return lax.ppermute(array, axis, [(i, size - 1 - i) for i in range(size)])  14.6 us
    ppermute x6, starting transfers between devices, swapped(): return lax.ppermute(array, 'head', [(0, 1), (1, 0)])  14.6 us
  transfers between devices with their start and end apart: 35, of which 18 were waited for; matrix products, arithmetic and copies ran while one was open for 8% of the time, Pallas kernels for 11%

profile of v3, /device:TPU:1, one launch (start us, length us, event | category | flops | bytes accessed | tf_op | source)
XLA Modules:
  0.0 217.0 jit_solution(4929934639392141198)
XLA Ops:
  2.3 9.0 %all-to-all-start = ((bf16[8,128,256]{2,1,0:T(8,128)(2,1)}), bf16[8,128,256]{2,1,0:T(8,128)(2,1)S(1)}, u32[]{:S(2)}, u32[]{:S(2)}) async-start(bf16[8,128,256]{2,1,0:T(8,128)(2,1)} %broadcast_in_dim.15), calls=%async_computation | async-start | bytes 1048576 | tf_op jit(solution)/shard_map/all_to_all | solution.py:44
  11.5 3.0 %collective-permute-start.1 = (bf16[256,512]{1,0:T(8,128)(2,1)S(1)}, bf16[256,512]{1,0:T(8,128)(2,1)}, u32[]{:S(2)}, u32[]{:S(2)}) collective-permute-start(bf16[256,512]{1,0:T(8,128)(2,1)S(1)} %get-tuple-element.97), channel_id=1, source_target_pairs={{0,1},{1,33},{16,0},{17,32},{32,17},{33,49},{48,16},{49,48},{2,3},... | collective-permute-start | bytes 786440 | tf_op jit(solution)/shard_map/ppermute | solution.py:352
  14.5 2.8 %collective-permute-start = (bf16[256,512]{1,0:T(8,128)(2,1)S(1)}, bf16[256,512]{1,0:T(8,128)(2,1)S(1)}, u32[]{:S(2)}, u32[]{:S(2)}) collective-permute-start(bf16[256,512]{1,0:T(8,128)(2,1)S(1)} %get-tuple-element.98), channel_id=1, source_target_pairs={{0,0},{1,32},{16,1},{17,33},{32,16},{33,48},{48,17},{49,49},{2,2},... | collective-permute-start | bytes 786440 | tf_op jit(solution)/shard_map/ppermute | solution.py:352
  42.0 5.4 %collective-permute-done.8 = bf16[256,256]{1,0:T(8,128)(2,1)} collective-permute-done((bf16[256,256]{1,0:T(8,128)(2,1)S(1)}, bf16[256,256]{1,0:T(8,128)(2,1)}, u32[]{:S(2)}, u32[]{:S(2)}) %collective-permute-start.8) | collective-permute-done | bytes 131104 | tf_op jit(solution)/shard_map/ppermute | solution.py:30
  49.2 7.0 %all-to-all-start.1 = ((bf16[8,128,256]{2,1,0:T(8,128)(2,1)}), bf16[8,128,256]{2,1,0:T(8,128)(2,1)}, u32[]{:S(2)}, u32[]{:S(2)}) async-start(bf16[8,128,256]{2,1,0:T(8,128)(2,1)} %broadcast_in_dim.16), calls=%async_computation.1 | async-start | bytes 1048576 | tf_op jit(solution)/shard_map/all_to_all | solution.py:44
  56.4 14.6 %collective-permute-done.11.noisy = bf16[128,2304]{1,0:T(8,128)(2,1)} collective-permute-done((bf16[128,2304]{1,0:T(8,128)(2,1)S(1)}, bf16[128,2304]{1,0:T(8,128)(2,1)}, u32[]{:S(2)}, u32[]{:S(2)}) %collective-permute-start.11) | collective-permute-done | bytes 589856 | tf_op jit(solution)/shard_map/ppermute | solution.py:35
  72.8 2.7 %collective-permute-start.14 = (bf16[1024,256]{1,0:T(8,128)(2,1)}, bf16[1024,256]{1,0:T(8,128)(2,1)S(1)}, u32[]{:S(2)}, u32[]{:S(2)}) collective-permute-start(bf16[1024,256]{1,0:T(8,128)(2,1)} %bitcast.7.kv_0), channel_id=1, source_target_pairs={{0,48},{16,0},{32,16},{48,32},{1,49},{17,1},{33,17},{49,33},{2,50}... | collective-permute-start | bytes 1572872 | tf_op jit(solution)/shard_map/ppermute | solution.py:30
  75.4 10.1 %collective-permute-done.12.kv_1 = bf16[1024,256]{1,0:T(8,128)(2,1)S(1)} collective-permute-done((bf16[1024,256]{1,0:T(8,128)(2,1)}, bf16[1024,256]{1,0:T(8,128)(2,1)S(1)}, u32[]{:S(2)}, u32[]{:S(2)}) %collective-permute-start.12) | collective-permute-done | bytes 524320 | tf_op jit(solution)/shard_map/ppermute | solution.py:30
  85.7 2.7 %collective-permute-start.15 = (bf16[512,256]{1,0:T(8,128)(2,1)S(1)}, bf16[512,256]{1,0:T(8,128)(2,1)}, u32[]{:S(2)}, u32[]{:S(2)}) collective-permute-start(bf16[512,256]{1,0:T(8,128)(2,1)S(1)} %slice.59), channel_id=1, source_target_pairs={{0,48},{16,0},{32,16},{48,32},{1,49},{17,1},{33,17},{49,33},{2,50}... | collective-permute-start | bytes 786440 | tf_op jit(solution)/shard_map/ppermute | solution.py:30
  95.1 20.0 %shard_map.93 = (bf16[128,1024]{1,0:T(8,128)(2,1)}, bf16[128,1280]{1,0:T(8,128)(2,1)}, bf16[1024,256]{1,0:T(8,128)(2,1)}, bf16[1024,256]{1,0:T(8,128)(2,1)}, bf1...) custom-call(s32[4]{0:T(128)} %pad_add_fusion.info, ...), custom_call_target="tpu_custom_call" | custom-call | flops 6000000000 | bytes 8000000 | tf_op jit(solution)/shard_map/pallas_call | solution.py:279
  117.8 4.0 %collective-permute-done.18 = bf16[512,256]{1,0:T(8,128)(2,1)S(1)} collective-permute-done((bf16[512,256]{1,0:T(8,128)(2,1)}, bf16[512,256]{1,0:T(8,128)(2,1)S(1)}, u32[]{:S(2)}, u32[]{:S(2)}) %collective-permute-start.18) | collective-permute-done | bytes 262176 | tf_op jit(solution)/shard_map/ppermute | solution.py:30
  124.1 2.7 %collective-permute-start.21 = (bf16[1024,256]{1,0:T(8,128)(2,1)S(1)}, bf16[1024,256]{1,0:T(8,128)(2,1)S(1)}, u32[]{:S(2)}, u32[]{:S(2)}) collective-permute-start(bf16[1024,256]{1,0:T(8,128)(2,1)S(1)} %add_convert_fusion.1), channel_id=1, source_target_pairs={{0,48},{16,0},{32,16},{48,32},{1,49},{17,1},{33,17},{49,33},{2,50}... | collective-permute-start | bytes 1572872 | tf_op jit(solution)/shard_map/ppermute | solution.py:30
  126.8 5.7 %collective-permute-done.19 = bf16[1024,256]{1,0:T(8,128)(2,1)S(1)} collective-permute-done((bf16[1024,256]{1,0:T(8,128)(2,1)S(1)}, bf16[1024,256]{1,0:T(8,128)(2,1)S(1)}, u32[]{:S(2)}, u32[]{:S(2)}) %collective-permute-start.19) | collective-permute-done | bytes 524320 | tf_op jit(solution)/shard_map/ppermute | solution.py:30
  134.0 9.5 %all-to-all-start.2 = ((bf16[8,128,256]{2,1,0:T(8,128)(2,1)}), bf16[8,128,256]{2,1,0:T(8,128)(2,1)S(1)}, u32[]{:S(2)}, u32[]{:S(2)}) async-start(bf16[8,128,256]{2,1,0:T(8,128)(2,1)} %bitcast.11), calls=%async_computation.2 | async-start | bytes 1048576 | tf_op jit(solution)/shard_map/all_to_all | solution.py:72
  143.4 3.0 %collective-permute-start.22 = (bf16[128,1280]{1,0:T(8,128)(2,1)}, bf16[128,1280]{1,0:T(8,128)(2,1)S(1)}, u32[]{:S(2)}, u32[]{:S(2)}) collective-permute-start(bf16[128,1280]{1,0:T(8,128)(2,1)} %get-tuple-element.74), channel_id=1, source_target_pairs={{0,48},{16,32},{32,16},{48,0},{1,49},{17,33},{33,17},{49,1},{2,50}... | collective-permute-start | bytes 983048 | tf_op jit(solution)/shard_map/ppermute | solution.py:35
  149.9 5.7 %all-to-all-done.2 = bf16[8,128,256]{2,1,0:T(8,128)(2,1)S(1)} async-done(((bf16[8,128,256]{2,1,0:T(8,128)(2,1)}), bf16[8,128,256]{2,1,0:T(8,128)(2,1)S(1)}, u32[]{:S(2)}, u32[]{:S(2)}) %all-to-all-start.2) | async-done | bytes 524320 | tf_op jit(solution)/shard_map/all_to_all | solution.py:72
  156.1 4.1 %collective-permute-start.26 = (bf16[256,256]{1,0:T(8,128)(2,1)S(1)}, bf16[256,256]{1,0:T(8,128)(2,1)S(1)}, u32[]{:S(2)}, u32[]{:S(2)}) collective-permute-start(bf16[256,256]{1,0:T(8,128)(2,1)S(1)} %get-tuple-element.84), channel_id=1, source_target_pairs={{0,32},{16,48},{32,0},{48,16},{1,33},{17,49},{33,1},{49,17},{2,34}... | collective-permute-start | bytes 393224 | tf_op jit(solution)/shard_map/ppermute | solution.py:30
  161.0 3.1 %shard_map.94 = (bf16[2,1024,256]{2,1,0:T(8,128)(2,1)}, bf16[2,1024,256]{2,1,0:T(8,128)(2,1)}) custom-call(s32[2]{0:T(128)} %pad_add_fusion.1.info, bf16[1024,256]{1,0:T(8,128)(2,1)} %bitcast.44, bf16[1024,256]{1,0:T(8,128)(2,1)} %copy-done.1, bf16[512,256]{1,0:T(8,128)(2,1)} %copy-done.7, bf16[512,256]{1,0:T(8,128)(2,1)} %copy-done.8, ...), custom_call_target="tpu_custom_call" | custom-call | tf_op jit(solution)/shard_map/pallas_call | solution.py:336
  166.5 11.7 %collective-permute-start.29 = (bf16[2,1024,256]{2,1,0:T(8,128)(2,1)}, bf16[2,1024,256]{2,1,0:T(8,128)(2,1)}, u32[]{:S(2)}, u32[]{:S(2)}) collective-permute-start(bf16[2,1024,256]{2,1,0:T(8,128)(2,1)} %get-tuple-element.87), channel_id=1, source_target_pairs={{0,1},{1,0},{2,3},{3,2},{4,5},{5,4},{6,7},{7,6},{8,9},{9,8},{10,11... | collective-permute-start | bytes 3145736 | tf_op jit(solution)/shard_map/ppermute | solution.py:39
  180.8 6.9 %all-to-all-start.3 = ((bf16[8,128,256]{2,1,0:T(8,128)(2,1)}), bf16[8,128,256]{2,1,0:T(8,128)(2,1)S(1)}, u32[]{:S(2)}, u32[]{:S(2)}) async-start(bf16[8,128,256]{2,1,0:T(8,128)(2,1)} %bitcast.19), calls=%async_computation.3 | async-start | bytes 1048576 | tf_op jit(solution)/shard_map/all_to_all | solution.py:72
  190.6 15.2 %all-to-all-done.3 = bf16[8,128,256]{2,1,0:T(8,128)(2,1)S(1)} async-done(((bf16[8,128,256]{2,1,0:T(8,128)(2,1)}), bf16[8,128,256]{2,1,0:T(8,128)(2,1)S(1)}, u32[]{:S(2)}, u32[]{:S(2)}) %all-to-all-start.3) | async-done | bytes 524320 | tf_op jit(solution)/shard_map/all_to_all | solution.py:72
  206.6 4.0 %all-to-all-start.4 = ((bf16[4,128,256]{2,1,0:T(8,128)(2,1)}), bf16[4,128,256]{2,1,0:T(8,128)(2,1)S(1)}, u32[]{:S(2)}, u32[]{:S(2)}) async-start(bf16[4,128,256]{2,1,0:T(8,128)(2,1)} %broadcast_in_dim.19), calls=%async_computation.4 | async-start | bytes 524288 | tf_op jit(solution)/shard_map/all_to_all | solution.py:439
  210.6 2.7 %fusion = bf16[256,2048]{1,0:T(8,128)(2,1)} fusion(f32[256,2048]{1,0:T(8,128)S(1)} %fusion.10, bf16[256,256]{1,0:T(8,128)(2,1)S(1)} %collective-permute-done.28, bf16[2048,256]{1,0:T(8,128)(2,1)} %bitcast.20), kind=kOutput, calls=%fused_computation.1 | convolution fusion | flops 269484032 | bytes 4325376 | tf_op jit(solution)/shard_map/dot_general | solution.py:444
  213.2 3.0 %all-to-all-done.4 = bf16[4,128,256]{2,1,0:T(8,128)(2,1)S(1)} async-done(((bf16[4,128,256]{2,1,0:T(8,128)(2,1)}), bf16[4,128,256]{2,1,0:T(8,128)(2,1)S(1)}, u32[]{:S(2)}, u32[]{:S(2)}) %all-to-all-start.4) | async-done | bytes 262176 | tf_op jit(solution)/shard_map/all_to_all | solution.py:439
  (119 shorter events, 56.8 us)
Async XLA Ops:
  2.3 27.1 %all-to-all-start = ((bf16[8,128,256]{2,1,0:T(8,128)(2,1)}), bf16[8,128,256]{2,1,0:T(8,128)(2,1)S(1)}, u32[]{:S(2)}, u32[]{:S(2)}) async-start(bf16[8,128,256]{2,1,0:T(8,128)(2,1)} %broadcast_in_dim.15), calls=%async_computation | async-start | bytes 1048576 | tf_op jit(solution)/shard_map/all_to_all | solution.py:44
  11.5 10.3 %collective-permute-start.1 = (bf16[256,512]{1,0:T(8,128)(2,1)S(1)}, bf16[256,512]{1,0:T(8,128)(2,1)}, u32[]{:S(2)}, u32[]{:S(2)}) collective-permute-start(bf16[256,512]{1,0:T(8,128)(2,1)S(1)} %get-tuple-element.97), channel_id=1, source_target_pairs={{0,1},{1,33},{16,0},{17,32},{32,17},{33,49},{48,16},{49,48},{2,3},... | collective-permute-start | bytes 786440 | tf_op jit(solution)/shard_map/ppermute | solution.py:352
  14.5 9.7 %collective-permute-start = (bf16[256,512]{1,0:T(8,128)(2,1)S(1)}, bf16[256,512]{1,0:T(8,128)(2,1)S(1)}, u32[]{:S(2)}, u32[]{:S(2)}) collective-permute-start(bf16[256,512]{1,0:T(8,128)(2,1)S(1)} %get-tuple-element.98), channel_id=1, source_target_pairs={{0,0},{1,32},{16,1},{17,33},{32,16},{33,48},{48,17},{49,49},{2,2},... | collective-permute-start | bytes 786440 | tf_op jit(solution)/shard_map/ppermute | solution.py:352
  17.2 9.4 %collective-permute-start.2 = (bf16[256,512]{1,0:T(8,128)(2,1)S(1)}, bf16[256,512]{1,0:T(8,128)(2,1)S(1)}, u32[]{:S(2)}, u32[]{:S(2)}) collective-permute-start(bf16[256,512]{1,0:T(8,128)(2,1)S(1)} %get-tuple-element.96), channel_id=1, source_target_pairs={{0,16},{1,48},{16,17},{17,49},{32,0},{33,32},{48,1},{49,33},{2,18}... | collective-permute-start | bytes 786440 | tf_op jit(solution)/shard_map/ppermute | solution.py:352
  19.7 9.8 %collective-permute-start.3 = (bf16[256,512]{1,0:T(8,128)(2,1)S(1)}, bf16[256,512]{1,0:T(8,128)(2,1)S(1)}, u32[]{:S(2)}, u32[]{:S(2)}) collective-permute-start(bf16[256,512]{1,0:T(8,128)(2,1)S(1)} %get-tuple-element.95), channel_id=1, source_target_pairs={{0,17},{1,49},{16,16},{17,48},{32,1},{33,33},{48,0},{49,32},{2,19}... | collective-permute-start | bytes 786440 | tf_op jit(solution)/shard_map/ppermute | solution.py:352
  38.5 8.9 %collective-permute-start.8 = (bf16[256,256]{1,0:T(8,128)(2,1)S(1)}, bf16[256,256]{1,0:T(8,128)(2,1)}, u32[]{:S(2)}, u32[]{:S(2)}) collective-permute-start(bf16[256,256]{1,0:T(8,128)(2,1)S(1)} %get-tuple-element.92), channel_id=1, source_target_pairs={{0,16},{16,32},{32,48},{48,0},{1,17},{17,33},{33,49},{49,1},{2,18}... | collective-permute-start | bytes 393224 | tf_op jit(solution)/shard_map/ppermute | solution.py:30
  38.5 8.9 %collective-permute-start.9 = (bf16[256,256]{1,0:T(8,128)(2,1)S(1)}, bf16[256,256]{1,0:T(8,128)(2,1)}, u32[]{:S(2)}, u32[]{:S(2)}) collective-permute-start(bf16[256,256]{1,0:T(8,128)(2,1)S(1)} %get-tuple-element.94), channel_id=1, source_target_pairs={{0,32},{16,48},{32,0},{48,16},{1,33},{17,49},{33,1},{49,17},{2,34}... | collective-permute-start | bytes 393224 | tf_op jit(solution)/shard_map/ppermute | solution.py:30
  49.2 23.5 %all-to-all-start.1 = ((bf16[8,128,256]{2,1,0:T(8,128)(2,1)}), bf16[8,128,256]{2,1,0:T(8,128)(2,1)}, u32[]{:S(2)}, u32[]{:S(2)}) async-start(bf16[8,128,256]{2,1,0:T(8,128)(2,1)} %broadcast_in_dim.16), calls=%async_computation.1 | async-start | bytes 1048576 | tf_op jit(solution)/shard_map/all_to_all | solution.py:44
  56.3 14.7 %collective-permute-start.11 = (bf16[128,2304]{1,0:T(8,128)(2,1)S(1)}, bf16[128,2304]{1,0:T(8,128)(2,1)}, u32[]{:S(2)}, u32[]{:S(2)}) collective-permute-start(bf16[128,2304]{1,0:T(8,128)(2,1)S(1)} %pad_maximum_fusion), channel_id=1, source_target_pairs={{0,48},{16,32},{32,16},{48,0},{1,49},{17,33},{33,17},{49,1},{2,50}... | collective-permute-start | bytes 1769480 | tf_op jit(solution)/shard_map/ppermute | solution.py:35
  72.8 12.8 %collective-permute-start.12 = (bf16[1024,256]{1,0:T(8,128)(2,1)}, bf16[1024,256]{1,0:T(8,128)(2,1)S(1)}, u32[]{:S(2)}, u32[]{:S(2)}) collective-permute-start(bf16[1024,256]{1,0:T(8,128)(2,1)} %bitcast.7.kv_0), channel_id=1, source_target_pairs={{0,16},{16,32},{32,48},{48,0},{1,17},{17,33},{33,49},{49,1},{2,18}... | collective-permute-start | bytes 1572872 | tf_op jit(solution)/shard_map/ppermute | solution.py:30
  72.8 12.9 %collective-permute-start.14 = (bf16[1024,256]{1,0:T(8,128)(2,1)}, bf16[1024,256]{1,0:T(8,128)(2,1)S(1)}, u32[]{:S(2)}, u32[]{:S(2)}) collective-permute-start(bf16[1024,256]{1,0:T(8,128)(2,1)} %bitcast.7.kv_0), channel_id=1, source_target_pairs={{0,48},{16,0},{32,16},{48,32},{1,49},{17,1},{33,17},{49,33},{2,50}... | collective-permute-start | bytes 1572872 | tf_op jit(solution)/shard_map/ppermute | solution.py:30
  92.1 22.9 %collective-permute-start.16 = (bf16[1024,256]{1,0:T(8,128)(2,1)S(1)}, bf16[1024,256]{1,0:T(8,128)(2,1)S(1)}, u32[]{:S(2)}, u32[]{:S(2)}) collective-permute-start(bf16[1024,256]{1,0:T(8,128)(2,1)S(1)} %bitcast.42), channel_id=1, source_target_pairs={{0,16},{16,32},{32,48},{48,0},{1,17},{17,33},{33,49},{49,1},{2,18}... | collective-permute-start | bytes 1572872 | tf_op jit(solution)/shard_map/ppermute | solution.py:30
  92.4 22.6 %collective-permute-start.17 = (bf16[1024,256]{1,0:T(8,128)(2,1)S(1)}, bf16[1024,256]{1,0:T(8,128)(2,1)S(1)}, u32[]{:S(2)}, u32[]{:S(2)}) collective-permute-start(bf16[1024,256]{1,0:T(8,128)(2,1)S(1)} %bitcast.43), channel_id=1, source_target_pairs={{0,48},{16,0},{32,16},{48,32},{1,49},{17,1},{33,17},{49,33},{2,50}... | collective-permute-start | bytes 1572872 | tf_op jit(solution)/shard_map/ppermute | solution.py:30
  122.9 9.6 %collective-permute-start.19 = (bf16[1024,256]{1,0:T(8,128)(2,1)S(1)}, bf16[1024,256]{1,0:T(8,128)(2,1)S(1)}, u32[]{:S(2)}, u32[]{:S(2)}) collective-permute-start(bf16[1024,256]{1,0:T(8,128)(2,1)S(1)} %add_convert_fusion.2), channel_id=1, source_target_pairs={{0,16},{16,32},{32,48},{48,0},{1,17},{17,33},{33,49},{49,1},{2,18}... | collective-permute-start | bytes 1572872 | tf_op jit(solution)/shard_map/ppermute | solution.py:30
  124.1 8.9 %collective-permute-start.21 = (bf16[1024,256]{1,0:T(8,128)(2,1)S(1)}, bf16[1024,256]{1,0:T(8,128)(2,1)S(1)}, u32[]{:S(2)}, u32[]{:S(2)}) collective-permute-start(bf16[1024,256]{1,0:T(8,128)(2,1)S(1)} %add_convert_fusion.1), channel_id=1, source_target_pairs={{0,48},{16,0},{32,16},{48,32},{1,49},{17,1},{33,17},{49,33},{2,50}... | collective-permute-start | bytes 1572872 | tf_op jit(solution)/shard_map/ppermute | solution.py:30
  134.0 21.6 %all-to-all-start.2 = ((bf16[8,128,256]{2,1,0:T(8,128)(2,1)}), bf16[8,128,256]{2,1,0:T(8,128)(2,1)S(1)}, u32[]{:S(2)}, u32[]{:S(2)}) async-start(bf16[8,128,256]{2,1,0:T(8,128)(2,1)} %bitcast.11), calls=%async_computation.2 | async-start | bytes 1048576 | tf_op jit(solution)/shard_map/all_to_all | solution.py:72
  143.4 12.3 %collective-permute-start.22 = (bf16[128,1280]{1,0:T(8,128)(2,1)}, bf16[128,1280]{1,0:T(8,128)(2,1)S(1)}, u32[]{:S(2)}, u32[]{:S(2)}) collective-permute-start(bf16[128,1280]{1,0:T(8,128)(2,1)} %get-tuple-element.74), channel_id=1, source_target_pairs={{0,48},{16,32},{32,16},{48,0},{1,49},{17,33},{33,17},{49,1},{2,50}... | collective-permute-start | bytes 983048 | tf_op jit(solution)/shard_map/ppermute | solution.py:35
  146.4 9.2 %collective-permute-start.23 = (bf16[512,256]{1,0:T(8,128)(2,1)S(1)}, bf16[512,256]{1,0:T(8,128)(2,1)S(1)}, u32[]{:S(2)}, u32[]{:S(2)}) collective-permute-start(bf16[512,256]{1,0:T(8,128)(2,1)S(1)} %slice.50), channel_id=1, source_target_pairs={{0,16},{16,32},{32,48},{48,0},{1,17},{17,33},{33,49},{49,1},{2,18}... | collective-permute-start | bytes 786440 | tf_op jit(solution)/shard_map/ppermute | solution.py:30
  147.2 8.4 %collective-permute-start.24 = (bf16[512,256]{1,0:T(8,128)(2,1)}, bf16[512,256]{1,0:T(8,128)(2,1)S(1)}, u32[]{:S(2)}, u32[]{:S(2)}) collective-permute-start(bf16[512,256]{1,0:T(8,128)(2,1)} %slice.51), channel_id=1, source_target_pairs={{0,48},{16,0},{32,16},{48,32},{1,49},{17,1},{33,17},{49,33},{2,50}... | collective-permute-start | bytes 786440 | tf_op jit(solution)/shard_map/ppermute | solution.py:30
  156.1 8.4 %collective-permute-start.26 = (bf16[256,256]{1,0:T(8,128)(2,1)S(1)}, bf16[256,256]{1,0:T(8,128)(2,1)S(1)}, u32[]{:S(2)}, u32[]{:S(2)}) collective-permute-start(bf16[256,256]{1,0:T(8,128)(2,1)S(1)} %get-tuple-element.84), channel_id=1, source_target_pairs={{0,32},{16,48},{32,0},{48,16},{1,33},{17,49},{33,1},{49,17},{2,34}... | collective-permute-start | bytes 393224 | tf_op jit(solution)/shard_map/ppermute | solution.py:30
  166.5 39.3 %collective-permute-start.29 = (bf16[2,1024,256]{2,1,0:T(8,128)(2,1)}, bf16[2,1024,256]{2,1,0:T(8,128)(2,1)}, u32[]{:S(2)}, u32[]{:S(2)}) collective-permute-start(bf16[2,1024,256]{2,1,0:T(8,128)(2,1)} %get-tuple-element.87), channel_id=1, source_target_pairs={{0,1},{1,0},{2,3},{3,2},{4,5},{5,4},{6,7},{7,6},{8,9},{9,8},{10,11... | collective-permute-start | bytes 3145736 | tf_op jit(solution)/shard_map/ppermute | solution.py:39
  180.8 25.0 %all-to-all-start.3 = ((bf16[8,128,256]{2,1,0:T(8,128)(2,1)}), bf16[8,128,256]{2,1,0:T(8,128)(2,1)S(1)}, u32[]{:S(2)}, u32[]{:S(2)}) async-start(bf16[8,128,256]{2,1,0:T(8,128)(2,1)} %bitcast.19), calls=%async_computation.3 | async-start | bytes 1048576 | tf_op jit(solution)/shard_map/all_to_all | solution.py:72
  188.6 22.0 %collective-permute-start.28 = (bf16[256,256]{1,0:T(8,128)(2,1)S(1)}, bf16[256,256]{1,0:T(8,128)(2,1)S(1)}, u32[]{:S(2)}, u32[]{:S(2)}) collective-permute-start(bf16[256,256]{1,0:T(8,128)(2,1)S(1)} %get-tuple-element.84), channel_id=1, source_target_pairs={{0,1},{1,0},{2,3},{3,2},{4,5},{5,4},{6,7},{7,6},{8,9},{9,8},{10,11... | collective-permute-start | bytes 393224 | tf_op jit(solution)/shard_map/ppermute | solution.py:39
  206.6 9.7 %all-to-all-start.4 = ((bf16[4,128,256]{2,1,0:T(8,128)(2,1)}), bf16[4,128,256]{2,1,0:T(8,128)(2,1)S(1)}, u32[]{:S(2)}, u32[]{:S(2)}) async-start(bf16[4,128,256]{2,1,0:T(8,128)(2,1)} %broadcast_in_dim.19), calls=%async_computation.4 | async-start | bytes 524288 | tf_op jit(solution)/shard_map/all_to_all | solution.py:439
  (24 other events, 282.2 us)
